TPU v7x, 256 devices: a whole 4x4x8 slice. The times are simulated.
256 devices in a mesh: dp: 64 (over z_hi, x, y, core), slab: 4 (over z_lo).
Axes of the slice: x: 4, y: 4, z: 8 (z_hi: 2, z_lo: 4; z = z_hi * 4 + z_lo), core: 2. Of those that a mesh axis runs over, the one named last changes fastest.
Arguments:
- images: bfloat16 [64, 256, 32, 128], P('dp', 'slab'), may hold values from -6 to 6
- cotangent: bfloat16 [64, 128, 64, 256], P('dp', None, 'slab'), may hold values from -6 to 6
- kernel: bfloat16 [3, 3, 256, 128], replicated, may hold values from -0.125 to 0.125
Outputs:
- grad_images: bfloat16 [64, 256, 32, 128], P('dp', 'slab')
- grad_kernel: float32 [3, 3, 256, 128], replicated
All inputs are finite; a program needn't handle non-finite values.
Results may differ from a plain program's by a relative error of at most 0.0034.
Values may be sent and summed in bfloat16 or wider, within the bound.
No kernel may reach another device: no remote copies, remote signals or barrier semaphores. Data moves between devices by JAX's collectives and lax.ppermute only.
A program may use at most 64 MiB of HBM per device.

v0:
```python
import jax
import jax.numpy as jnp
from jax import lax
from jax.sharding import PartitionSpec as P


def extended(cells, sides, width):
    for axis, dim in sides:
        count = lax.axis_size(axis)
        ends = count - 1
        head = lax.slice_in_dim(cells, 0, width, axis=dim)
        tail = lax.slice_in_dim(cells, cells.shape[dim] - width, cells.shape[dim], axis=dim)
        cells = jnp.concatenate(
            [
                lax.ppermute(tail, axis, [(i, (i + 1) % count) for i in range(ends)]),
                cells,
                lax.ppermute(head, axis, [((i + 1) % count, i) for i in range(ends)]),
            ],
            axis=dim,
        )
    return cells


def upsample(field):
    return jnp.repeat(jnp.repeat(field, 2, axis=2), 2, axis=3)


def downsum(field):
    count, chans, rows, cols = field.shape
    return field.reshape(count, chans, rows // 2, 2, cols // 2, 2).sum(axis=(3, 5))


def kernel_terms(padded_up, grad_rows):
    return lax.conv_general_dilated(
        padded_up,
        grad_rows,
        (1, 1),
        ((0, 0), (1, 1)),
        dimension_numbers=("CNHW", "IOHW", "HWNC"),
        preferred_element_type=jnp.float32,
    )


def input_terms(padded_grad, kernel):
    flipped = kernel[::-1, ::-1]
    return lax.conv_general_dilated(
        padded_grad,
        flipped,
        (1, 1),
        ((0, 0), (1, 1)),
        dimension_numbers=("NCHW", "HWOI", "NCHW"),
        preferred_element_type=jnp.float32,
    )


def body(images, cotangent, kernel):
    slab_up = lax.all_to_all(upsample(images), "slab", split_axis=2, concat_axis=1, tiled=True)
    padded_up = extended(slab_up, (("slab", 2),), 1)
    padded_grad = extended(cotangent, (("slab", 2),), 1)
    partial_kernel = kernel_terms(padded_up, cotangent)
    grad_low = downsum(input_terms(padded_grad, kernel))
    returned = lax.all_to_all(
        grad_low.astype(jnp.bfloat16), "slab", split_axis=1, concat_axis=2, tiled=True
    ).astype(grad_low.dtype)
    total = lax.psum(partial_kernel, ("dp", "slab"))
    return (returned.astype(jnp.bfloat16), total)


def solution(mesh):
    placed = (P("dp", "slab", None, None), P("dp", None, "slab", None), P())
    return jax.shard_map(
        body,
        mesh=mesh,
        in_specs=placed,
        out_specs=(P("dp", "slab", None, None), P()),
        check_vma=False,
    )
```

profile of v0, /device:TPU:6, one launch (start us, length us, event | category | flops | bytes accessed | tf_op | source)
XLA Modules:
  0.0 440.7 jit_solution(2120381636830538440)
XLA Ops:
  9.8 4.7 %copy.37 = bf16[64,64,128]{1,0,2:T(8,128)(2,1)S(1)} copy(bf16[64,64,128]{2,0,1:T(8,128)(2,1)} %bitcast.38) | data formatting | bytes 2097152 | tf_op jit(solution)/shard_map/broadcast_in_dim | solution.py:25
  14.5 3.3 broadcast_in_dim.12
  17.8 7.8 %copy.38 = bf16[1,64,64,256]{3,1,0,2:T(8,128)(2,1)} copy(bf16[1,64,64,256]{2,1,3,0:T(8,128)(2,1)} %bitcast.35) | data formatting | bytes 4194304 | tf_op jit(solution)/shard_map/broadcast_in_dim | solution.py:25
  25.6 5.9 %all-to-all-start.1 = ((bf16[1,64,64,256]{3,1,0,2:T(8,128)(2,1)}), bf16[1,64,64,256]{3,1,0,2:T(8,128)(2,1)S(1)}, u32[]{:S(2)}, u32[]{:S(2)}) async-start(bf16[1,64,64,256]{3,1,0,2:T(8,128)(2,1)} %copy.38), calls=%async_computation.1 | async-start | bytes 4194304 | tf_op jit(solution)/shard_map/all_to_all | solution.py:57
  32.9 3.9 collective-permute-start
  38.3 4.5 %copy.44 = bf16[1,128,16,256]{1,0,3,2:T(2,128)(2,1)} copy(bf16[1,128,16,256]{3,2,1,0:T(8,128)(2,1)} %param.4) | data formatting | bytes 2097152 | tf_op args[1]
  42.8 25.4 %collective-permute-done = bf16[1,128,1,256]{3,2,1,0:T(2,128)(2,1)S(1)} collective-permute-done((bf16[1,128,1,256]{3,2,1,0:T(2,128)(2,1)S(1)}, bf16[1,128,1,256]{3,2,1,0:T(2,128)(2,1)S(1)}, u32[]{:S(2)}, u32[]{:S(2)}) %collective-permute-start) | collective-permute-done | bytes 65568 | tf_op jit(solution)/shard_map/ppermute | solution.py:15
  68.2 3.4 maximum_bitcast_fusion
  71.6 2.7 copy.45
  74.3 2.6 pad.clone
  76.9 3.0 reshape.29
  81.5 3.0 broadcast_select_fusion
  84.5 3.3 copy.33
  89.2 5.1 %copy.41 = bf16[1,256,16,256]{1,0,3,2:T(2,128)(2,1)} copy(bf16[1,256,16,256]{3,2,1,0:T(8,128)(2,1)S(1)} %bitcast.36) | data formatting | bytes 4194304 | tf_op jit(solution)/shard_map/all_to_all | solution.py:57
  94.3 2.3 fusion.13
  96.6 17.5 %collective-permute-start.2 = (bf16[1,256,1,256]{1,0,3,2:T(2,128)(2,1)}, bf16[1,256,1,256]{1,0,3,2:T(2,128)(2,1)}, u32[]{:S(2)}, u32[]{:S(2)}) collective-permute-start(bf16[1,256,1,256]{1,0,3,2:T(2,128)(2,1)} %get-tuple-element.2), channel_id=1, source_target_pairs={{0,1},{1,2},{2,3},{4,5},{5,6},{6,7},{8,9},{9,10},{10,11},{12,13},{... | collective-permute-start | bytes 393224 | tf_op jit(solution)/shard_map/ppermute | solution.py:15
  115.6 4.6 %slice_bitcast_fusion = f32[1,256,16,256]{1,2,3,0:T(8,128)} fusion(f32[16,1,264,256]{3,0,2,1:T(8,128)} %bitcast.34), kind=kLoop, calls=%fused_computation.2 | loop fusion | bytes 8388608 | tf_op jit(solution)/shard_map/conv_general_dilated | solution.py:46
  120.2 5.8 %reshape.26 = f32[256,8,2,128,2]{0,2,1,4,3:T(2,128)} reshape(f32[1,256,16,256]{1,2,3,0:T(8,128)} %slice_bitcast_fusion) | data formatting | bytes 8388608 | tf_op jit(solution)/shard_map/reshape | solution.py:30
  126.0 5.9 %reduce_sum.9 = bf16[256,8,128]{0,1,2:T(8,128)(2,1)S(1)} reduce(f32[256,8,2,128,2]{0,2,1,4,3:T(2,128)} %reshape.26, f32[]{:T(128)} %constant.0.clone.1), dimensions={2,4}, to_apply=%region_0.0 | reduce | flops 786432 | bytes 4718596 | tf_op jit(solution)/shard_map/reduce_sum | solution.py:30
  133.2 4.2 all-to-all-start
  137.5 30.8 %fusion = f32[3,3,256,128]{3,2,1,0:T(8,128)} fusion(bf16[1,128,16,256]{1,0,3,2:T(2,128)(2,1)S(1)} %copy-done.1, bf16[1,256,1,256]{1,0,3,2:T(2,128)(2,1)} %collective-permute-done.3, bf16[1,256,16,256]{1,0,3,2:T(2,128)(2,1)} %copy.41, bf16[1,256,1,256]{1,0,3,2:T(2,128)(2,1)} %collective-permute-done.2), kind=kOutput, calls=%fused_computation.1 | convolution fusion | flops 2416705536 | bytes 4587520 | tf_op jit(solution)/shard_map/conv_general_dilated | solution.py:34
  168.3 1.9 copy.47
  170.2 261.3 %all-reduce.2.cloned.1.call-done = f32[3,3,256,128]{3,2,1,0:T(8,128)} async-done(((f32[3,3,256,128]{3,2,1,0:T(8,128)}), f32[3,3,256,128]{3,2,1,0:T(8,128)}) %all-reduce.2.cloned.1.call-update) | async-done | bytes 1179664 | tf_op jit(solution)/shard_map/psum | solution.py:65
  431.5 2.4 copy.49
  (23 shorter events, 11.3 us)
Async XLA Ops:
  7.2 74.3 %copy-start = (bf16[3,3,256,128]{3,2,1,0:T(8,128)(2,1)S(1)}, bf16[3,3,256,128]{3,2,1,0:T(8,128)(2,1)}, u32[]{:S(2)}) copy-start(bf16[3,3,256,128]{3,2,1,0:T(8,128)(2,1)} %param.5) | copy-start | bytes 1769476
  25.6 62.3 %all-to-all-start.1 = ((bf16[1,64,64,256]{3,1,0,2:T(8,128)(2,1)}), bf16[1,64,64,256]{3,1,0,2:T(8,128)(2,1)S(1)}, u32[]{:S(2)}, u32[]{:S(2)}) async-start(bf16[1,64,64,256]{3,1,0,2:T(8,128)(2,1)} %copy.38), calls=%async_computation.1 | async-start | bytes 4194304 | tf_op jit(solution)/shard_map/all_to_all | solution.py:57
  32.9 35.3 %collective-permute-start = (bf16[1,128,1,256]{3,2,1,0:T(2,128)(2,1)S(1)}, bf16[1,128,1,256]{3,2,1,0:T(2,128)(2,1)S(1)}, u32[]{:S(2)}, u32[]{:S(2)}) collective-permute-start(bf16[1,128,1,256]{3,2,1,0:T(2,128)(2,1)S(1)} %get-tuple-element.4), channel_id=1, source_target_pairs={{0,1},{1,2},{2,3},{4,5},{5,6},{6,7},{8,9},{9,10},{10,11},{12,13},{... | collective-permute-start | bytes 196616 | tf_op jit(solution)/shard_map/ppermute | solution.py:15
  36.8 31.4 %collective-permute-start.1 = (bf16[1,128,1,256]{3,2,1,0:T(2,128)(2,1)S(1)}, bf16[1,128,1,256]{3,2,1,0:T(2,128)(2,1)S(1)}, u32[]{:S(2)}, u32[]{:S(2)}) collective-permute-start(bf16[1,128,1,256]{3,2,1,0:T(2,128)(2,1)S(1)} %get-tuple-element.5), channel_id=1, source_target_pairs={{1,0},{2,1},{3,2},{5,4},{6,5},{7,6},{9,8},{10,9},{11,10},{13,12},{... | collective-permute-start | bytes 196616 | tf_op jit(solution)/shard_map/ppermute | solution.py:17
  76.9 4.6 %copy-start.2 = (pred[8,33]{0,1:T(8,128)(4,1)S(1)}, pred[8,33]{0,1:T(8,128)(4,1)}, u32[]{:S(2)}) copy-start(pred[8,33]{0,1:T(8,128)(4,1)} %constant.8) | copy-start | bytes 796
  96.6 40.8 %collective-permute-start.2 = (bf16[1,256,1,256]{1,0,3,2:T(2,128)(2,1)}, bf16[1,256,1,256]{1,0,3,2:T(2,128)(2,1)}, u32[]{:S(2)}, u32[]{:S(2)}) collective-permute-start(bf16[1,256,1,256]{1,0,3,2:T(2,128)(2,1)} %get-tuple-element.2), channel_id=1, source_target_pairs={{0,1},{1,2},{2,3},{4,5},{5,6},{6,7},{8,9},{9,10},{10,11},{12,13},{... | collective-permute-start | bytes 393224 | tf_op jit(solution)/shard_map/ppermute | solution.py:15
  114.1 23.4 %collective-permute-start.3 = (bf16[1,256,1,256]{1,0,3,2:T(2,128)(2,1)S(1)}, bf16[1,256,1,256]{1,0,3,2:T(2,128)(2,1)}, u32[]{:S(2)}, u32[]{:S(2)}) collective-permute-start(bf16[1,256,1,256]{1,0,3,2:T(2,128)(2,1)S(1)} %get-tuple-element.3), channel_id=1, source_target_pairs={{1,0},{2,1},{3,2},{5,4},{6,5},{7,6},{9,8},{10,9},{11,10},{13,12},{... | collective-permute-start | bytes 393224 | tf_op jit(solution)/shard_map/ppermute | solution.py:17
  126.0 11.5 %copy-start.1 = (bf16[1,128,16,256]{1,0,3,2:T(2,128)(2,1)S(1)}, bf16[1,128,16,256]{1,0,3,2:T(2,128)(2,1)}, u32[]{:S(2)}) copy-start(bf16[1,128,16,256]{1,0,3,2:T(2,128)(2,1)} %copy.44) | copy-start | bytes 3145732
  133.2 35.0 %all-to-all-start = ((bf16[1,256,8,128]{3,2,0,1:T(8,128)(2,1)}), bf16[1,256,8,128]{3,2,0,1:T(8,128)(2,1)}, u32[]{:S(2)}, u32[]{:S(2)}) async-start(bf16[1,256,8,128]{3,2,0,1:T(8,128)(2,1)} %copy.34), calls=%async_computation | async-start | bytes 1048576 | tf_op jit(solution)/shard_map/all_to_all | solution.py:62
  137.4 294.1 %all-reduce.2.cloned.1.call-start = ((), (), s32[]{:S(2)}) async-start(), calls=%async_computation.2 | async-start | bytes 2359296 | tf_op jit(solution)/shard_map/psum | solution.py:65
Sparse Core Ops, SparseCore 0:
  168.4 263.0 all-reduce.1
where the time goes:
time: 442 us; the launch traced here: 441 us
  waiting for transfers between devices  287 us (65%)
  local copies, waits for them, and re-layouts  62.3 us (14%)
  starting transfers between devices  34.5 us (8%)
  matrix products  33.8 us (8%)
  between operations  14.2 us (3%)
  other arithmetic  9.27 us (2%)
    psum x1, waiting for transfers between devices, body(): total = lax.psum(partial_kernel, ('dp', 'slab'))  261 us
    conv_general_dilated x1, matrix products, kernel_terms(): lax.conv_general_dilated(padded_up, grad_rows, (1, 1), ((0, 0), (1, 1)),...  30.8 us
    ppermute x2, waiting for transfers between devices, extended(): lax.ppermute(tail, axis, [(i, (i + 1) % count) for i in range(ends)])  25.4 us
    ppermute x2, starting transfers between devices, extended(): lax.ppermute(tail, axis, [(i, (i + 1) % count) for i in range(ends)])  21.4 us
    broadcast_in_dim x4, local copies, waits for them, and re-layouts, upsample(): return jnp.repeat(jnp.repeat(field, 2, axis=2), 2, axis=3)  17.1 us
    conv_general_dilated x5, local copies, waits for them, and re-layouts, input_terms(): lax.conv_general_dilated(padded_grad, flipped, (1, 1), ((0, 0), (1, 1)),...  12.5 us
    unnamed x9, local copies, waits for them, and re-layouts  9.55 us
  transfers between devices with their start and end apart: 7, of which 2 were waited for; matrix products, arithmetic and copies ran while one was open for 17% of the time, Pallas kernels for 0%

commit v1 on v0

v1 whole, which is shorter than its diff:
```python
import functools

import jax
import jax.numpy as jnp
from jax import lax
from jax.experimental import pallas as pl
from jax.experimental.pallas import tpu as pltpu
from jax.sharding import Mesh
from jax.sharding import PartitionSpec as P

BF = jnp.bfloat16
F32 = jnp.float32
NT = (((1,), (1,)), ((), ()))


def picker():
    col = lax.broadcasted_iota(jnp.int32, (256, 384), 0)
    n = lax.broadcasted_iota(jnp.int32, (256, 384), 1)
    start = 2 * (n & 127) + 1 - (n >> 7)
    return jnp.where((col == start) | (col == start + 1), 1.0, 0.0).astype(BF)


def stacked(wide):
    return jnp.concatenate([wide[:, 128 * b : 128 * b + 128] for b in range(3)], axis=0)


def pool_kernel(cot_ref, d_ref, y_ref):
    pick = picker()
    for i in range(8):
        part = jnp.dot(cot_ref[pl.ds(256 * i, 256), :], pick, preferred_element_type=F32)
        for b in range(3):
            y_ref[b, pl.ds(256 * i, 256), :] = part[:, 128 * b : 128 * b + 128]
    for b in range(3):
        above = None
        for p in range(8):
            even = y_ref[b, pl.ds(2 * p, 128, stride=16), :]
            odd = y_ref[b, pl.ds(2 * p + 1, 128, stride=16), :]
            upper = even if above is None else above + even
            d_ref[pl.ds(128 * (6 + b), 128), pl.ds(128 * p, 128)] = upper.astype(BF)
            d_ref[pl.ds(128 * (3 + b), 128), pl.ds(128 * p, 128)] = (even + odd).astype(BF)
            if p > 0:
                d_ref[pl.ds(128 * b, 128), pl.ds(128 * (p - 1), 128)] = upper.astype(BF)
            above = odd
        d_ref[pl.ds(128 * b, 128), pl.ds(896, 128)] = above.astype(BF)


def products(pixels, d_ref, edge_ref, out_ref):
    for k in range(0, 9, 3):
        part = lax.dot_general(pixels, d_ref[pl.ds(128 * k, 384), :], NT, preferred_element_type=F32)
        if k != 3:
            p = 7 if k == 0 else 0
            edge = edge_ref[pl.ds(64 * k, 384), :]
            part += lax.dot_general(
                pixels[:, 128 * p : 128 * p + 128], edge, NT, preferred_element_type=F32
            )
        for u in range(3):
            out_ref[pl.ds(128 * (k + u), 128), :] = part[:, 128 * u : 128 * u + 128]


def rows_of(m_ref, half):
    return m_ref[pl.ds(pl.multiple_of(half * 128, 128), 128), :]


def send_kernel(core_ref, img_ref, d_ref, top_ref, bot_ref, send_ref, m_ref, edge_ref, f_ref):
    pick = picker()
    edge_ref[pl.ds(0, 384), :] = stacked(jnp.dot(bot_ref[...], pick, preferred_element_type=F32)).astype(BF)
    edge_ref[pl.ds(384, 384), :] = stacked(jnp.dot(top_ref[...], pick, preferred_element_type=F32)).astype(BF)
    f_ref[...] = img_ref[...].astype(F32)
    for p in range(8):
        m_ref[:, pl.ds(128 * p, 128)] = f_ref[pl.ds(p, 256, stride=8), :].astype(BF)
    products(rows_of(m_ref, 1 - core_ref[0]), d_ref, edge_ref, send_ref)


def keep_kernel(core_ref, m_ref, d_ref, edge_ref, keep_ref):
    products(rows_of(m_ref, core_ref[0]), d_ref, edge_ref, keep_ref)


def join_kernel(keep_ref, came_ref, half_ref):
    half_ref[...] = (keep_ref[...] + came_ref[...]).astype(BF)


def fold_kernel(count, copies, x_ref, out_ref):
    rows = x_ref.shape[0] // count
    total = x_ref[pl.ds(0, rows), :].astype(F32)
    for k in range(1, count):
        total += x_ref[pl.ds(rows * k, rows), :].astype(F32)
    total = total.astype(out_ref.dtype)
    for k in range(copies):
        out_ref[pl.ds(rows * k, rows), :] = total


def image_kernel(slab_ref, ker_ref, d_ref, top_ref, bot_ref, *refs):
    f_ref = refs[4]
    pick = picker()
    edges = {
        0: (6, stacked(jnp.dot(top_ref[...], pick, preferred_element_type=F32)).astype(BF)),
        7: (0, stacked(jnp.dot(bot_ref[...], pick, preferred_element_type=F32)).astype(BF)),
    }
    weights = jnp.concatenate([ker_ref[k] for k in range(9)], axis=1)
    for h in range(4):
        part = jnp.dot(weights, d_ref[:, pl.ds(256 * h, 256)], preferred_element_type=F32)
        for p in (2 * h, 2 * h + 1):
            cells = part[:, 128 * (p % 2) : 128 * (p % 2) + 128]
            if p in edges:
                k, edge = edges[p]
                cells += jnp.dot(weights[:, 128 * k : 128 * k + 384], edge, preferred_element_type=F32)
            f_ref[pl.ds(p, 256, stride=8), :] = cells
    for k in range(4):
        place = pl.multiple_of((slab_ref[0] ^ k) * 512, 512)
        refs[k][...] = f_ref[pl.ds(place, 512), :].astype(BF)


def call(kernel, outs, scratch, flops, scalars, *args):
    spec = pl.BlockSpec(memory_space=pltpu.VMEM)
    ins = [pl.BlockSpec(memory_space=pltpu.SMEM)] * scalars + [spec] * (len(args) - scalars)
    sizes = sum(a.size * a.dtype.itemsize for a in args) + sum(o.size * o.dtype.itemsize for o in outs)
    return pl.pallas_call(
        kernel,
        out_shape=tuple(outs),
        in_specs=ins,
        out_specs=tuple([spec] * len(outs)),
        scratch_shapes=scratch,
        compiler_params=pltpu.CompilerParams(vmem_limit_bytes=24 << 20),
        cost_estimate=pl.CostEstimate(flops=flops, bytes_accessed=sizes, transcendentals=0),
    )(*args)


SWAP = [(0, 1), (1, 0)]
DOWN = [(0, 1), (1, 2), (2, 3)]
UP = [(1, 0), (2, 1), (3, 2)]


def fold(x, copies, dtype):
    count, rows, lanes = x.shape
    (out,) = call(
        functools.partial(fold_kernel, count, copies),
        [jax.ShapeDtypeStruct((copies * rows, lanes), dtype)], [], x.size, 0, x.reshape(count * rows, lanes),
    )
    return out.reshape(copies, rows, lanes)


def exchange(x, axes):
    return lax.all_to_all(x, axes, split_axis=0, concat_axis=0, tiled=True)


def body(images, cotangent, kernel):
    S = jax.ShapeDtypeStruct
    cot = cotangent[0]
    top = lax.ppermute(cot[:, 15, :], "s", DOWN)
    bot = lax.ppermute(cot[:, 0, :], "s", UP)
    blocks = images.reshape(64, 4, 8, 128).transpose(1, 0, 2, 3)
    img = exchange(blocks, "s").reshape(2048, 128)
    (d,) = call(
        pool_kernel, [S((1152, 1024), BF)],
        [pltpu.VMEM((3, 2048, 128), F32)], 450000000, 0, cot.reshape(2048, 256),
    )
    core, slab = lax.axis_index("c"), lax.axis_index("s")
    place = core.reshape(1).astype(jnp.int32)
    send, pixels, edges = call(
        send_kernel, [S((1152, 128), F32), S((256, 1024), BF), S((768, 128), BF)],
        [pltpu.VMEM((2048, 128), F32)], 300000000, 1, place, img, d, top, bot,
    )
    (keep,) = call(keep_kernel, [S((1152, 128), F32)], [], 300000000, 1, place, pixels, d, edges)
    low = call(
        image_kernel, [S((512, 128), BF)] * 4, [pltpu.VMEM((2048, 128), F32)],
        600000000, 1, slab.reshape(1).astype(jnp.int32), kernel.reshape(9, 256, 128), d, top, bot,
    )
    across = lax.axis_size("x") * lax.axis_size("y")
    along = lax.axis_size("zh") * lax.axis_size("s")
    rows = 1152 // across
    came = lax.ppermute(send, "c", SWAP)
    (half,) = call(join_kernel, [S((1152, 128), BF)], [], 150000, 0, keep, came)
    half = exchange(half.reshape(across, rows, 128), ("x", "y"))
    part = fold(half, along, F32)
    part = exchange(part, ("zh", "s"))
    part = fold(part, across, BF)
    mine = exchange(part, ("x", "y"))
    mine = mine.reshape(9, 128, 128)
    other = lax.ppermute(mine, "c", SWAP)
    first = core == 0
    total = jnp.concatenate([jnp.where(first, mine, other), jnp.where(first, other, mine)], axis=1)
    came = [low[0]] + [
        lax.ppermute(low[k], "s", [(i, i ^ k) for i in range(4)]) for k in (1, 2, 3)
    ]
    came = [x.reshape(64, 8, 128) for x in came]
    tiles = []
    for i in range(4):
        k = slab ^ i
        tiles.append(
            jnp.where(k == 0, came[0], jnp.where(k == 1, came[1], jnp.where(k == 2, came[2], came[3])))
        )
    grad_low = jnp.stack(tiles, axis=1).reshape(1, 64, 32, 128)
    return grad_low, total.astype(F32).reshape(3, 3, 256, 128)


def solution(mesh):
    fine = Mesh(mesh.devices.reshape(2, 4, 4, 2, 4), ("zh", "x", "y", "c", "s"))
    dp = ("zh", "x", "y", "c")
    placed = (P(dp, "s", None, None), P(dp, None, "s", None), P())
    return jax.shard_map(
        body,
        mesh=fine,
        in_specs=placed,
        out_specs=(P(dp, "s", None, None), P()),
        check_vma=False,
    )
```

time: 442 us -> 84.3 us (0.19)
  waiting for transfers between devices: 287 us -> 13.1 us
  local copies, waits for them, and re-layouts: 62.3 us -> 5.63 us
  matrix products: 33.8 us -> 0 us
  blocking collectives: 0 us -> 32.3 us
  between operations: 14.2 us -> 0.75 us
  starting transfers between devices: 34.5 us -> 21.3 us
  Pallas kernels: 0 us -> 6.66 us
  other arithmetic: 9.27 us -> 4 us
    psum x1 -> x0, waiting for transfers between devices: 261 us -> none  [body(): total = lax.psum(partial_kernel, ('dp', 'slab'))]
    conv_general_dilated x2 -> x0, matrix products: 33.8 us -> none  [the longest x1 30.8 us: kernel_terms(): lax.conv_general_dilated(padded_up, grad_rows, (1, 1), ((0, 0), (1, 1)),...]
    all_to_all x0 -> x2, blocking collectives: none -> 32.3 us  [exchange(): return lax.all_to_all(x, axes, split_axis=0, concat_axis=0, tiled=True)]
    broadcast_in_dim x4 -> x0, local copies, waits for them, and re-layouts: 17.1 us -> none  [upsample(): return jnp.repeat(jnp.repeat(field, 2, axis=2), 2, axis=3)]
    ppermute x4 -> x7, waiting for transfers between devices: 25.4 us -> 9.48 us  [the longest x3 5.94 us: body(): lax.ppermute(low[k], 's', [(i, i ^ k) for i in range(4)])]
    ppermute x4 -> x7, starting transfers between devices: 24.4 us -> 9.69 us  [the longest x3 4.39 us: body(): lax.ppermute(low[k], 's', [(i, i ^ k) for i in range(4)])]
    conv_general_dilated x5 -> x0, local copies, waits for them, and re-layouts: 12.5 us -> none  [input_terms(): lax.conv_general_dilated(padded_grad, flipped, (1, 1), ((0, 0), (1, 1)),...]
    all_to_all x4 -> x0, local copies, waits for them, and re-layouts: 8.39 us -> none  [the longest x3 6.46 us: body(): lax.all_to_all(upsample(images), 'slab', split_axis=2, concat_axis=1, til...]
  transfers between devices with their start and end apart: 7 -> 9, of which waited for: 2 -> 6; matrix products, arithmetic and copies ran while one was open for 17% -> 3% of each run, Pallas kernels for 0% -> 5%
where the time goes in v1:
time: 84.3 us; the launch traced here: 83.7 us
  blocking collectives  32.3 us (38%)
  starting transfers between devices  21.3 us (25%)
  waiting for transfers between devices  13.1 us (16%)
  Pallas kernels  6.66 us (8%)
  local copies, waits for them, and re-layouts  5.63 us (7%)
  other arithmetic  4 us (5%)
    all_to_all x2, blocking collectives, exchange(): return lax.all_to_all(x, axes, split_axis=0, concat_axis=0, tiled=True)  32.3 us
    all_to_all x2, starting transfers between devices, exchange(): return lax.all_to_all(x, axes, split_axis=0, concat_axis=0, tiled=True)  11.6 us
    pallas_call x7, Pallas kernels, call(): pl.pallas_call(kernel, out_shape=tuple(outs), in_specs=ins, out_specs=tup...  6.66 us
    ppermute x3, waiting for transfers between devices, body(): lax.ppermute(low[k], 's', [(i, i ^ k) for i in range(4)])  5.94 us
    ppermute x3, starting transfers between devices, body(): lax.ppermute(low[k], 's', [(i, i ^ k) for i in range(4)])  4.39 us
    unnamed x15, local copies, waits for them, and re-layouts  4.09 us
    ppermute x1, starting transfers between devices, body(): top = lax.ppermute(cot[:, 15, :], 's', DOWN)  3.92 us
    all_to_all x2, waiting for transfers between devices, exchange(): return lax.all_to_all(x, axes, split_axis=0, concat_axis=0, tiled=True)  3.63 us
  transfers between devices with their start and end apart: 9, of which 6 were waited for; matrix products, arithmetic and copies ran while one was open for 3% of the time, Pallas kernels for 5%

profile of v1, /device:TPU:6, one launch (start us, length us, event | category | flops | bytes accessed | tf_op | source)
XLA Modules:
  0.0 83.7 jit_solution(5142884278072222874)
XLA Ops:
  0.7 1.0 %copy-done = bf16[1,64,32,128]{3,2,1,0:T(8,128)(2,1)S(1)} copy-done((bf16[1,64,32,128]{3,2,1,0:T(8,128)(2,1)S(1)}, bf16[1,64,32,128]{3,2,1,0:T(8,128)(2,1)}, u32[]{:S(2)}) %copy-start) | copy-done | bytes 524312
  1.7 0.9 %copy_bitcast_fusion.1 = bf16[4,64,8,128]{3,2,1,0:T(8,128)(2,1)} fusion(bf16[1,64,32,128]{3,2,1,0:T(8,128)(2,1)S(1)} %copy-done), kind=kLoop, calls=%fused_computation.3 | loop fusion | bytes 1048576 | tf_op jit(solution)/shard_map/transpose | solution.py:151
  2.6 5.9 %all-to-all-start = ((bf16[4,64,8,128]{3,2,1,0:T(8,128)(2,1)}), bf16[4,64,8,128]{3,2,1,0:T(8,128)(2,1)S(1)}, u32[]{:S(2)}, u32[]{:S(2)}) async-start(bf16[4,64,8,128]{3,2,1,0:T(8,128)(2,1)} %copy_bitcast_fusion.1), calls=%async_computation | async-start | bytes 1048576 | tf_op jit(solution)/shard_map/all_to_all | solution.py:143
  9.5 3.9 %collective-permute-start = (bf16[128,256]{1,0:T(8,128)(2,1)}, bf16[128,256]{1,0:T(8,128)(2,1)S(1)}, u32[]{:S(2)}, u32[]{:S(2)}) collective-permute-start(bf16[128,256]{1,0:T(8,128)(2,1)} %get-tuple-element.17), channel_id=1, source_target_pairs={{0,1},{1,2},{2,3},{4,5},{5,6},{6,7},{8,9},{9,10},{10,11},{12,13},{... | collective-permute-start | bytes 196616 | tf_op jit(solution)/shard_map/ppermute | solution.py:149
  13.4 1.3 %collective-permute-start.1 = (bf16[128,256]{1,0:T(8,128)(2,1)}, bf16[128,256]{1,0:T(8,128)(2,1)S(1)}, u32[]{:S(2)}, u32[]{:S(2)}) collective-permute-start(bf16[128,256]{1,0:T(8,128)(2,1)} %get-tuple-element.16), channel_id=1, source_target_pairs={{1,0},{2,1},{3,2},{5,4},{6,5},{7,6},{9,8},{10,9},{11,10},{13,12},{... | collective-permute-start | bytes 196616 | tf_op jit(solution)/shard_map/ppermute | solution.py:150
  14.7 1.2 %copy-done.2 = bf16[1,128,16,256]{3,2,1,0:T(8,128)(2,1)S(1)} copy-done((bf16[1,128,16,256]{3,2,1,0:T(8,128)(2,1)S(1)}, bf16[1,128,16,256]{3,2,1,0:T(8,128)(2,1)}, u32[]{:S(2)}) %copy-start.2) | copy-done | bytes 1048600
  15.9 1.7 %shard_map.50.d_ref = bf16[1152,1024]{1,0:T(8,128)(2,1)S(1)} custom-call(bf16[2048,256]{1,0:T(8,128)(2,1)S(1)} %bitcast.35), custom_call_target="tpu_custom_call" | custom-call | flops 450000000 | bytes 3407872 | tf_op jit(solution)/shard_map/pallas_call | solution.py:117
  17.6 1.0 %collective-permute-done.top_ref = bf16[128,256]{1,0:T(8,128)(2,1)S(1)} collective-permute-done((bf16[128,256]{1,0:T(8,128)(2,1)}, bf16[128,256]{1,0:T(8,128)(2,1)S(1)}, u32[]{:S(2)}, u32[]{:S(2)}) %collective-permute-start) | collective-permute-done | bytes 65568 | tf_op jit(solution)/shard_map/ppermute | solution.py:149
  18.6 1.4 %collective-permute-done.1.bot_ref = bf16[128,256]{1,0:T(8,128)(2,1)S(1)} collective-permute-done((bf16[128,256]{1,0:T(8,128)(2,1)}, bf16[128,256]{1,0:T(8,128)(2,1)S(1)}, u32[]{:S(2)}, u32[]{:S(2)}) %collective-permute-start.1) | collective-permute-done | bytes 65568 | tf_op jit(solution)/shard_map/ppermute | solution.py:150
  20.0 3.6 %all-to-all-done = bf16[4,64,8,128]{3,2,1,0:T(8,128)(2,1)S(1)} async-done(((bf16[4,64,8,128]{3,2,1,0:T(8,128)(2,1)}), bf16[4,64,8,128]{3,2,1,0:T(8,128)(2,1)S(1)}, u32[]{:S(2)}, u32[]{:S(2)}) %all-to-all-start) | async-done | bytes 524320 | tf_op jit(solution)/shard_map/all_to_all | solution.py:143
  23.6 1.3 %shard_map.52 = (f32[1152,128]{1,0:T(8,128)S(1)}, bf16[256,1024]{1,0:T(8,128)(2,1)S(1)}, bf16[768,128]{1,0:T(8,128)(2,1)S(1)}) custom-call(s32[1]{0:T(128)} %bitcast.11.core_ref, bf16[2048,128]{1,0:T(8,128)(2,1)S(1)} %bitcast.36, bf16[1152,1024]{1,0:T(8,128)(2,1)S(1)} %shard_map.50.d_ref, bf16[128,256]{1,0:T(8,128)(2,1)S(1)} %collective-permute-done.top_ref, ...), custom_call_target="tpu_custom_call" | custom-call | flops 300000000 | bytes 4325380 | tf_op jit(solution)/shard_map/pallas_call | solution.py:117
  25.1 0.9 %shard_map.53.keep_ref = f32[1152,128]{1,0:T(8,128)S(1)} custom-call(s32[1]{0:T(128)} %bitcast.11.core_ref, bf16[256,1024]{1,0:T(8,128)(2,1)S(1)} %get-tuple-element.13.m_ref, bf16[1152,1024]{1,0:T(8,128)(2,1)S(1)} %shard_map.50.d_ref, bf16[768,128]{1,0:T(8,128)(2,1)S(1)} %get-tuple-element.14.edge_ref), custom_call_target="tpu_custom_call" | custom-call | flops 300000000 | bytes 3670020 | tf_op jit(solution)/shard_map/pallas_call | solution.py:117
  25.9 1.1 %collective-permute-done.5.came_ref = f32[1152,128]{1,0:T(8,128)S(1)} collective-permute-done((f32[1152,128]{1,0:T(8,128)S(1)}, f32[1152,128]{1,0:T(8,128)S(1)}, u32[]{:S(2)}, u32[]{:S(2)}) %collective-permute-start.5) | collective-permute-done | bytes 589856 | tf_op jit(solution)/shard_map/ppermute | solution.py:171
  27.1 14.3 %all_to_all.20 = bf16[16,72,128]{2,1,0:T(8,128)(2,1)S(1)} all-to-all(bf16[16,72,128]{2,1,0:T(8,128)(2,1)S(1)} %bitcast.40), channel_id=1, replica_groups=mesh['zh'=2,'x'=4,'y'=4,'c'=2,'s'=4] {'x','y'}, dimensions={0} | all-to-all | bytes 589824 | tf_op jit(solution)/shard_map/all_to_all | solution.py:143
  41.4 18.0 %all_to_all.21 = f32[8,72,128]{2,1,0:T(8,128)S(1)} all-to-all(f32[8,72,128]{2,1,0:T(8,128)S(1)} %bitcast.38), channel_id=1, replica_groups=mesh['zh'=2,'x'=4,'y'=4,'c'=2,'s'=4] {'zh','s'}, dimensions={0} | all-to-all | bytes 589824 | tf_op jit(solution)/shard_map/all_to_all | solution.py:143
  60.2 5.7 %all-to-all-start.3 = ((bf16[16,72,128]{2,1,0:T(8,128)(2,1)}), bf16[16,72,128]{2,1,0:T(8,128)(2,1)}, u32[]{:S(2)}, u32[]{:S(2)}) async-start(bf16[16,72,128]{2,1,0:T(8,128)(2,1)} %bitcast.19), calls=%async_computation.3 | async-start | bytes 589824 | tf_op jit(solution)/shard_map/all_to_all | solution.py:143
  66.7 2.0 %shard_map.51 = (bf16[512,128]{1,0:T(8,128)(2,1)S(1)}, bf16[512,128]{1,0:T(8,128)(2,1)}, bf16[512,128]{1,0:T(8,128)(2,1)}, bf16[512,128]{1,0:T(8,128)(2,1)}) custom-call(s32[1]{0:T(128)} %bitcast.slab_ref, bf16[9,256,128]{2,1,0:T(8,128)(2,1)S(1)} %bitcast.41, bf16[1152,1024]{1,0:T(8,128)(2,1)S(1)} %shard_map.50.d_ref, ...), custom_call_target="tpu_custom_call" | custom-call | flops 600000000 | bytes 3604484 | tf_op jit(solution)/shard_map/pallas_call | solution.py:117
  70.4 3.3 %collective-permute-start.4 = (bf16[512,128]{1,0:T(8,128)(2,1)}, bf16[512,128]{1,0:T(8,128)(2,1)S(1)}, u32[]{:S(2)}, u32[]{:S(2)}) collective-permute-start(bf16[512,128]{1,0:T(8,128)(2,1)} %get-tuple-element.12), channel_id=1, source_target_pairs={{0,3},{1,2},{2,1},{3,0},{4,7},{5,6},{6,5},{7,4},{8,11},{9,10},{10,... | collective-permute-start | bytes 393224 | tf_op jit(solution)/shard_map/ppermute | solution.py:183
  73.7 2.2 %collective-permute-done.2 = bf16[512,128]{1,0:T(8,128)(2,1)S(1)} collective-permute-done((bf16[512,128]{1,0:T(8,128)(2,1)}, bf16[512,128]{1,0:T(8,128)(2,1)S(1)}, u32[]{:S(2)}, u32[]{:S(2)}) %collective-permute-start.2) | collective-permute-done | bytes 131104 | tf_op jit(solution)/shard_map/ppermute | solution.py:183
  76.0 3.7 %collective-permute-done.3 = bf16[512,128]{1,0:T(8,128)(2,1)S(1)} collective-permute-done((bf16[512,128]{1,0:T(8,128)(2,1)}, bf16[512,128]{1,0:T(8,128)(2,1)S(1)}, u32[]{:S(2)}, u32[]{:S(2)}) %collective-permute-start.3) | collective-permute-done | bytes 131104 | tf_op jit(solution)/shard_map/ppermute | solution.py:183
  79.7 1.0 %select_bitcast_fusion.3 = (bf16[64,1,8,128]{3,2,0,1:T(8,128)(2,1)S(1)}, bf16[64,1,8,128]{3,2,0,1:T(8,128)(2,1)S(1)}, bf16[64,1,8,128]{3,2,0,1:T(8,128)(2,1)S(1)}, bf16[64,1,8,128]{3,2,0,1:T(8,128)(2,1)S(1)}) fusion(bf16[512,128]{1,0:T(8,128)(2,1)} %copy-done.6, bf16[512,128]{1,0:T(8,128)(2,1)S(1)} %collective-permute-done.2, ...), kind=kLoop, calls=%fused_computation.10 | loop fusion | flops 786432 | bytes 1048588 | tf_op jit(solution)/shard_map/jit(_where)/select_n | solution.py:190
  80.7 0.9 %copy_bitcast_fusion.2 = bf16[1,64,32,128]{3,2,1,0:T(8,128)(2,1)} fusion(bf16[64,1,8,128]{3,2,0,1:T(8,128)(2,1)S(1)} %get-tuple-element.21, bf16[64,1,8,128]{3,2,0,1:T(8,128)(2,1)S(1)} %get-tuple-element.22, bf16[64,1,8,128]{3,2,0,1:T(8,128)(2,1)S(1)} %get-tuple-element.23, bf16[64,1,8,128]{3,2,0,1:T(8,128)(2,1)S(1)} %get-tuple-element.20), kind=kLoop, calls=%fused_computation.4 | loop fusion | flops 786432 | bytes 1048576 | tf_op jit(solution)/shard_map/reshape | solution.py:192
  81.6 1.0 %broadcast_select_fusion.1 = (bf16[9,128,128]{2,1,0:T(8,128)(2,1)S(1)}, bf16[9,128,128]{2,1,0:T(8,128)(2,1)S(1)}) fusion(bf16[9,128,128]{2,1,0:T(8,128)(2,1)} %bitcast.20, bf16[9,128,128]{2,1,0:T(8,128)(2,1)S(1)} %collective-permute-done.6, pred[]{:T(512)S(6)} %eq.51), kind=kLoop, calls=%fused_computation.6 | loop fusion | flops 294912 | bytes 1179649 | tf_op jit(solution)/shard_map/jit(_where)/select_n | solution.py:181
  82.6 1.1 %maximum_convert_fusion = f32[3,3,256,128]{3,2,1,0:T(8,128)} fusion(bf16[3,3,128,128]{3,2,1,0:T(8,128)(2,1)S(1)} %bitcast.44, bf16[3,3,128,128]{3,2,1,0:T(8,128)(2,1)S(1)} %bitcast.43), kind=kLoop, calls=%fused_computation.1 | loop fusion | flops 1179648 | bytes 1769472 | tf_op jit(solution)/shard_map/convert_element_type | solution.py:193
  (24 shorter events, 4.5 us)
Async XLA Ops:
  0.6 1.0 %copy-start = (bf16[1,64,32,128]{3,2,1,0:T(8,128)(2,1)S(1)}, bf16[1,64,32,128]{3,2,1,0:T(8,128)(2,1)}, u32[]{:S(2)}) copy-start(bf16[1,64,32,128]{3,2,1,0:T(8,128)(2,1)} %param.3) | copy-start | bytes 1572868
  0.6 7.8 %copy-start.1 = (bf16[1,128,16,256]{3,2,1,0:T(8,128)(2,1)S(1)}, bf16[1,128,16,256]{3,2,1,0:T(8,128)(2,1)}, u32[]{:S(2)}) copy-start(bf16[1,128,16,256]{3,2,1,0:T(8,128)(2,1)} %param.4) | copy-start | bytes 3145732
  2.6 21.1 %all-to-all-start = ((bf16[4,64,8,128]{3,2,1,0:T(8,128)(2,1)}), bf16[4,64,8,128]{3,2,1,0:T(8,128)(2,1)S(1)}, u32[]{:S(2)}, u32[]{:S(2)}) async-start(bf16[4,64,8,128]{3,2,1,0:T(8,128)(2,1)} %copy_bitcast_fusion.1), calls=%async_computation | async-start | bytes 1048576 | tf_op jit(solution)/shard_map/all_to_all | solution.py:143
  9.5 9.1 %collective-permute-start = (bf16[128,256]{1,0:T(8,128)(2,1)}, bf16[128,256]{1,0:T(8,128)(2,1)S(1)}, u32[]{:S(2)}, u32[]{:S(2)}) collective-permute-start(bf16[128,256]{1,0:T(8,128)(2,1)} %get-tuple-element.17), channel_id=1, source_target_pairs={{0,1},{1,2},{2,3},{4,5},{5,6},{6,7},{8,9},{9,10},{10,11},{12,13},{... | collective-permute-start | bytes 196616 | tf_op jit(solution)/shard_map/ppermute | solution.py:149
  13.4 6.6 %collective-permute-start.1 = (bf16[128,256]{1,0:T(8,128)(2,1)}, bf16[128,256]{1,0:T(8,128)(2,1)S(1)}, u32[]{:S(2)}, u32[]{:S(2)}) collective-permute-start(bf16[128,256]{1,0:T(8,128)(2,1)} %get-tuple-element.16), channel_id=1, source_target_pairs={{1,0},{2,1},{3,2},{5,4},{6,5},{7,6},{9,8},{10,9},{11,10},{13,12},{... | collective-permute-start | bytes 196616 | tf_op jit(solution)/shard_map/ppermute | solution.py:150
  14.7 1.2 %copy-start.2 = (bf16[1,128,16,256]{3,2,1,0:T(8,128)(2,1)S(1)}, bf16[1,128,16,256]{3,2,1,0:T(8,128)(2,1)}, u32[]{:S(2)}) copy-start(bf16[1,128,16,256]{3,2,1,0:T(8,128)(2,1)} %param.4) | copy-start | bytes 3145732
  20.0 4.9 %copy-start.4 = (bf16[128,256]{1,0:T(8,128)(2,1)}, bf16[128,256]{1,0:T(8,128)(2,1)S(1)}, u32[]{:S(2)}) copy-start(bf16[128,256]{1,0:T(8,128)(2,1)S(1)} %collective-permute-done.1.bot_ref) | copy-start | bytes 196612
  25.0 2.1 %collective-permute-start.5 = (f32[1152,128]{1,0:T(8,128)S(1)}, f32[1152,128]{1,0:T(8,128)S(1)}, u32[]{:S(2)}, u32[]{:S(2)}) collective-permute-start(f32[1152,128]{1,0:T(8,128)S(1)} %get-tuple-element.15), channel_id=1, source_target_pairs={{0,4},{4,0},{1,5},{5,1},{2,6},{6,2},{3,7},{7,3},{8,12},{12,8},{9,1... | collective-permute-start | bytes 1769480 | tf_op jit(solution)/shard_map/ppermute | solution.py:171
  41.4 24.5 %copy-start.3 = (bf16[3,3,256,128]{3,2,1,0:T(8,128)(2,1)S(1)}, bf16[3,3,256,128]{3,2,1,0:T(8,128)(2,1)}, u32[]{:S(2)}) copy-start(bf16[3,3,256,128]{3,2,1,0:T(8,128)(2,1)} %param.5) | copy-start | bytes 1769476
  60.2 13.6 %all-to-all-start.3 = ((bf16[16,72,128]{2,1,0:T(8,128)(2,1)}), bf16[16,72,128]{2,1,0:T(8,128)(2,1)}, u32[]{:S(2)}, u32[]{:S(2)}) async-start(bf16[16,72,128]{2,1,0:T(8,128)(2,1)} %bitcast.19), calls=%async_computation.3 | async-start | bytes 589824 | tf_op jit(solution)/shard_map/all_to_all | solution.py:143
  65.9 0.8 %copy-start.5 = (bf16[128,256]{1,0:T(8,128)(2,1)S(1)}, bf16[128,256]{1,0:T(8,128)(2,1)}, u32[]{:S(2)}) copy-start(bf16[128,256]{1,0:T(8,128)(2,1)} %copy-done.4) | copy-start | bytes 196612
  68.7 0.7 copy-start.6
  69.4 6.6 %collective-permute-start.2 = (bf16[512,128]{1,0:T(8,128)(2,1)}, bf16[512,128]{1,0:T(8,128)(2,1)S(1)}, u32[]{:S(2)}, u32[]{:S(2)}) collective-permute-start(bf16[512,128]{1,0:T(8,128)(2,1)} %get-tuple-element.10), channel_id=1, source_target_pairs={{0,1},{1,0},{2,3},{3,2},{4,5},{5,4},{6,7},{7,6},{8,9},{9,8},{10,11... | collective-permute-start | bytes 393224 | tf_op jit(solution)/shard_map/ppermute | solution.py:183
  69.9 9.8 %collective-permute-start.3 = (bf16[512,128]{1,0:T(8,128)(2,1)}, bf16[512,128]{1,0:T(8,128)(2,1)S(1)}, u32[]{:S(2)}, u32[]{:S(2)}) collective-permute-start(bf16[512,128]{1,0:T(8,128)(2,1)} %get-tuple-element.11), channel_id=1, source_target_pairs={{0,2},{1,3},{2,0},{3,1},{4,6},{5,7},{6,4},{7,5},{8,10},{9,11},{10,... | collective-permute-start | bytes 393224 | tf_op jit(solution)/shard_map/ppermute | solution.py:183
  70.4 9.2 %collective-permute-start.4 = (bf16[512,128]{1,0:T(8,128)(2,1)}, bf16[512,128]{1,0:T(8,128)(2,1)S(1)}, u32[]{:S(2)}, u32[]{:S(2)}) collective-permute-start(bf16[512,128]{1,0:T(8,128)(2,1)} %get-tuple-element.12), channel_id=1, source_target_pairs={{0,3},{1,2},{2,1},{3,0},{4,7},{5,6},{6,5},{7,4},{8,11},{9,10},{10,... | collective-permute-start | bytes 393224 | tf_op jit(solution)/shard_map/ppermute | solution.py:183
  73.7 7.8 %collective-permute-start.6 = (bf16[9,128,128]{2,1,0:T(8,128)(2,1)}, bf16[9,128,128]{2,1,0:T(8,128)(2,1)S(1)}, u32[]{:S(2)}, u32[]{:S(2)}) collective-permute-start(bf16[9,128,128]{2,1,0:T(8,128)(2,1)} %bitcast.20), channel_id=1, source_target_pairs={{0,4},{4,0},{1,5},{5,1},{2,6},{6,2},{3,7},{7,3},{8,12},{12,8},{9,1... | collective-permute-start | bytes 884744 | tf_op jit(solution)/shard_map/ppermute | solution.py:179

commit v2 on v1

--- a/solution.py
+++ b/solution.py
@@ -61,11 +61,26 @@
     return m_ref[pl.ds(pl.multiple_of(half * 128, 128), 128), :]
 
 
-def send_kernel(core_ref, img_ref, d_ref, top_ref, bot_ref, send_ref, m_ref, edge_ref, f_ref):
+def part_kernel(slab_ref, images_ref, *refs):
+    sems = refs[4]
+    copies = []
+    for k in (3, 2, 1, 0):
+        place = pl.multiple_of((slab_ref[0] ^ k) * 8, 8)
+        copy = pltpu.make_async_copy(images_ref.at[:, pl.ds(place, 8), :], refs[k], sems.at[k])
+        copy.start()
+        copies.append(copy)
+    for copy in copies:
+        copy.wait()
+
+
+def send_kernel(core_ref, slab_ref, *refs):
+    d_ref, top_ref, bot_ref, send_ref, m_ref, edge_ref, f_ref = refs[4:]
     pick = picker()
     edge_ref[pl.ds(0, 384), :] = stacked(jnp.dot(bot_ref[...], pick, preferred_element_type=F32)).astype(BF)
     edge_ref[pl.ds(384, 384), :] = stacked(jnp.dot(top_ref[...], pick, preferred_element_type=F32)).astype(BF)
-    f_ref[...] = img_ref[...].astype(F32)
+    for k in range(4):
+        place = pl.multiple_of((slab_ref[0] ^ k) * 512, 512)
+        f_ref[pl.ds(place, 512), :] = refs[k][...].astype(F32)
     for p in range(8):
         m_ref[:, pl.ds(128 * p, 128)] = f_ref[pl.ds(p, 256, stride=8), :].astype(BF)
     products(rows_of(m_ref, 1 - core_ref[0]), d_ref, edge_ref, send_ref)
@@ -139,6 +154,10 @@
     return out.reshape(copies, rows, lanes)
 
 
+def swapped(x, k):
+    return lax.ppermute(x, "s", [(i, i ^ k) for i in range(4)])
+
+
 def exchange(x, axes):
     return lax.all_to_all(x, axes, split_axis=0, concat_axis=0, tiled=True)
 
@@ -146,24 +165,34 @@
 def body(images, cotangent, kernel):
     S = jax.ShapeDtypeStruct
     cot = cotangent[0]
+    core = lax.axis_index("c").reshape(1).astype(jnp.int32)
+    slab = lax.axis_index("s").reshape(1).astype(jnp.int32)
+    blocks = pl.pallas_call(
+        part_kernel,
+        out_shape=(S((64, 8, 128), BF),) * 4,
+        in_specs=[pl.BlockSpec(memory_space=pltpu.SMEM), pl.BlockSpec(memory_space=pltpu.HBM)],
+        out_specs=(pl.BlockSpec(memory_space=pltpu.VMEM),) * 4,
+        scratch_shapes=[pltpu.SemaphoreType.DMA((4,))],
+        compiler_params=pltpu.CompilerParams(vmem_limit_bytes=8 << 20),
+        cost_estimate=pl.CostEstimate(flops=0, bytes_accessed=1048576, transcendentals=0),
+        name="parted",
+    )(slab, images[0])
+    img = {k: swapped(blocks[k], k) for k in (3, 2, 1)}
+    img = [x.reshape(512, 128) for x in (blocks[0], img[1], img[2], img[3])]
     top = lax.ppermute(cot[:, 15, :], "s", DOWN)
     bot = lax.ppermute(cot[:, 0, :], "s", UP)
-    blocks = images.reshape(64, 4, 8, 128).transpose(1, 0, 2, 3)
-    img = exchange(blocks, "s").reshape(2048, 128)
     (d,) = call(
         pool_kernel, [S((1152, 1024), BF)],
         [pltpu.VMEM((3, 2048, 128), F32)], 450000000, 0, cot.reshape(2048, 256),
     )
-    core, slab = lax.axis_index("c"), lax.axis_index("s")
-    place = core.reshape(1).astype(jnp.int32)
     send, pixels, edges = call(
         send_kernel, [S((1152, 128), F32), S((256, 1024), BF), S((768, 128), BF)],
-        [pltpu.VMEM((2048, 128), F32)], 300000000, 1, place, img, d, top, bot,
-    )
-    (keep,) = call(keep_kernel, [S((1152, 128), F32)], [], 300000000, 1, place, pixels, d, edges)
+        [pltpu.VMEM((2048, 128), F32)], 300000000, 2, core, slab, *img, d, top, bot,
+    )
+    (keep,) = call(keep_kernel, [S((1152, 128), F32)], [], 300000000, 1, core, pixels, d, edges)
     low = call(
         image_kernel, [S((512, 128), BF)] * 4, [pltpu.VMEM((2048, 128), F32)],
-        600000000, 1, slab.reshape(1).astype(jnp.int32), kernel.reshape(9, 256, 128), d, top, bot,
+        600000000, 1, slab, kernel.reshape(9, 256, 128), d, top, bot,
     )
     across = lax.axis_size("x") * lax.axis_size("y")
     along = lax.axis_size("zh") * lax.axis_size("s")
@@ -177,15 +206,15 @@
     mine = exchange(part, ("x", "y"))
     mine = mine.reshape(9, 128, 128)
     other = lax.ppermute(mine, "c", SWAP)
-    first = core == 0
+    first = core[0] == 0
     total = jnp.concatenate([jnp.where(first, mine, other), jnp.where(first, other, mine)], axis=1)
-    came = [low[0]] + [
-        lax.ppermute(low[k], "s", [(i, i ^ k) for i in range(4)]) for k in (1, 2, 3)
-    ]
+    came = [low[0]]
+    for k in (1, 2, 3):
+        came.append(swapped(low[k], k))
     came = [x.reshape(64, 8, 128) for x in came]
     tiles = []
     for i in range(4):
-        k = slab ^ i
+        k = slab[0] ^ i
         tiles.append(
             jnp.where(k == 0, came[0], jnp.where(k == 1, came[1], jnp.where(k == 2, came[2], came[3])))
         )

time: 84.3 us -> 80.4 us (0.954)
  waiting for transfers between devices: 13.1 us -> 10.2 us
  starting transfers between devices: 21.3 us -> 19 us
  blocking collectives: 32.3 us -> 34.2 us
  Pallas kernels: 6.66 us -> 8.53 us
  local copies, waits for them, and re-layouts: 5.63 us -> 4 us
  other arithmetic: 4 us -> 3.1 us
    all_to_all x2 -> x1, starting transfers between devices: 11.6 us -> 5.7 us  [exchange(): return lax.all_to_all(x, axes, split_axis=0, concat_axis=0, tiled=True)]
    ppermute x3 -> x6, starting transfers between devices: 4.39 us -> 9.58 us  [swapped(): return lax.ppermute(x, 's', [(i, i ^ k) for i in range(4)])]
    all_to_all x2 -> x1, waiting for transfers between devices: 3.63 us -> 0.39 us  [exchange(): return lax.all_to_all(x, axes, split_axis=0, concat_axis=0, tiled=True)]
    all_to_all x2, blocking collectives: 32.3 us -> 34.2 us  [exchange(): return lax.all_to_all(x, axes, split_axis=0, concat_axis=0, tiled=True)]
    ppermute x1, waiting for transfers between devices: 1.43 us -> 3.35 us  [body(): bot = lax.ppermute(cot[:, 0, :], 's', UP)]
    ppermute x1, starting transfers between devices: 3.92 us -> 2.37 us  [body(): top = lax.ppermute(cot[:, 15, :], 's', DOWN)]
    pallas_call x7, Pallas kernels: 6.66 us -> 7.66 us  [call(): pl.pallas_call(kernel, out_shape=tuple(outs), in_specs=ins, out_specs=tup...]
    ppermute x1, waiting for transfers between devices: 1 us -> 0.01 us  [body(): top = lax.ppermute(cot[:, 15, :], 's', DOWN)]
  transfers between devices with their start and end apart: 9 -> 11, of which waited for: 6 -> 5; matrix products, arithmetic and copies ran while one was open for 3% -> 4% of each run, Pallas kernels for 5% -> 6%
where the time goes in v2:
time: 80.4 us; the launch traced here: 79.9 us
  blocking collectives  34.2 us (43%)
  starting transfers between devices  19 us (24%)
  waiting for transfers between devices  10.2 us (13%)
  Pallas kernels  8.53 us (11%)
  local copies, waits for them, and re-layouts  4 us (5%)
  other arithmetic  3.1 us (4%)
    all_to_all x2, blocking collectives, exchange(): return lax.all_to_all(x, axes, split_axis=0, concat_axis=0, tiled=True)  34.2 us
    ppermute x6, starting transfers between devices, swapped(): return lax.ppermute(x, 's', [(i, i ^ k) for i in range(4)])  9.58 us
    pallas_call x7, Pallas kernels, call(): pl.pallas_call(kernel, out_shape=tuple(outs), in_specs=ins, out_specs=tup...  7.66 us
    all_to_all x1, starting transfers between devices, exchange(): return lax.all_to_all(x, axes, split_axis=0, concat_axis=0, tiled=True)  5.7 us
    ppermute x6, waiting for transfers between devices, swapped(): return lax.ppermute(x, 's', [(i, i ^ k) for i in range(4)])  5.35 us
    ppermute x1, waiting for transfers between devices, body(): bot = lax.ppermute(cot[:, 0, :], 's', UP)  3.35 us
    unnamed x11, local copies, waits for them, and re-layouts  3.34 us
    ppermute x1, starting transfers between devices, body(): top = lax.ppermute(cot[:, 15, :], 's', DOWN)  2.37 us
  transfers between devices with their start and end apart: 11, of which 5 were waited for; matrix products, arithmetic and copies ran while one was open for 4% of the time, Pallas kernels for 6%

profile of v2, /device:TPU:6, one launch (start us, length us, event | category | flops | bytes accessed | tf_op | source)
XLA Modules:
  0.0 79.9 jit_solution(3904951398070654230)
XLA Ops:
  0.6 1.0 %copy-done.2 = bf16[1,64,32,128]{3,2,1,0:T(8,128)(2,1)S(1)} copy-done((bf16[1,64,32,128]{3,2,1,0:T(8,128)(2,1)S(1)}, bf16[1,64,32,128]{3,2,1,0:T(8,128)(2,1)}, u32[]{:S(2)}) %copy-start.2) | copy-done | bytes 524312
  1.7 0.9 %parted.1 = (bf16[64,8,128]{2,1,0:T(8,128)(2,1)S(1)}, bf16[64,8,128]{2,1,0:T(8,128)(2,1)}, bf16[64,8,128]{2,1,0:T(8,128)(2,1)}, bf16[64,8,128]{2,1,0:T(8,128)(2,1)}) custom-call(s32[1]{0:T(128)} %bitcast.slab_ref, bf16[64,32,128]{2,1,0:T(8,128)(2,1)S(1)} %bitcast.40), custom_call_target="tpu_custom_call" | custom-call | bytes 1048576 | tf_op jit(solution)/shard_map/parted/pallas_call | solution.py:170
  3.2 1.9 %collective-permute-start.5 = (bf16[64,8,128]{2,1,0:T(8,128)(2,1)}, bf16[64,8,128]{2,1,0:T(8,128)(2,1)}, u32[]{:S(2)}, u32[]{:S(2)}) collective-permute-start(bf16[64,8,128]{2,1,0:T(8,128)(2,1)} %get-tuple-element.18), channel_id=1, source_target_pairs={{0,1},{1,0},{2,3},{3,2},{4,5},{5,4},{6,7},{7,6},{8,9},{9,8},{10,11... | collective-permute-start | bytes 393224 | tf_op jit(solution)/shard_map/ppermute | solution.py:158
  5.1 3.3 %collective-permute-start.6 = (bf16[64,8,128]{2,1,0:T(8,128)(2,1)}, bf16[64,8,128]{2,1,0:T(8,128)(2,1)}, u32[]{:S(2)}, u32[]{:S(2)}) collective-permute-start(bf16[64,8,128]{2,1,0:T(8,128)(2,1)} %get-tuple-element.19), channel_id=1, source_target_pairs={{0,2},{1,3},{2,0},{3,1},{4,6},{5,7},{6,4},{7,5},{8,10},{9,11},{10,... | collective-permute-start | bytes 393224 | tf_op jit(solution)/shard_map/ppermute | solution.py:158
  8.4 1.6 %copy.9 = bf16[1,128,16,256]{3,1,2,0:T(8,128)(2,1)S(1)} copy(bf16[1,128,16,256]{3,2,1,0:T(8,128)(2,1)} %param.4) | data formatting | bytes 2097152 | tf_op args[1]
  10.1 0.7 slice_bitcast_fusion
  10.7 2.4 %collective-permute-start = (bf16[128,256]{1,0:T(8,128)(2,1)}, bf16[128,256]{1,0:T(8,128)(2,1)S(1)}, u32[]{:S(2)}, u32[]{:S(2)}) collective-permute-start(bf16[128,256]{1,0:T(8,128)(2,1)} %get-tuple-element.25), channel_id=1, source_target_pairs={{0,1},{1,2},{2,3},{4,5},{5,6},{6,7},{8,9},{9,10},{10,11},{12,13},{... | collective-permute-start | bytes 196616 | tf_op jit(solution)/shard_map/ppermute | solution.py:182
  13.1 1.3 %collective-permute-start.1 = (bf16[128,256]{1,0:T(8,128)(2,1)}, bf16[128,256]{1,0:T(8,128)(2,1)S(1)}, u32[]{:S(2)}, u32[]{:S(2)}) collective-permute-start(bf16[128,256]{1,0:T(8,128)(2,1)} %get-tuple-element.24), channel_id=1, source_target_pairs={{1,0},{2,1},{3,2},{5,4},{6,5},{7,6},{9,8},{10,9},{11,10},{13,12},{... | collective-permute-start | bytes 196616 | tf_op jit(solution)/shard_map/ppermute | solution.py:183
  14.4 1.7 %shard_map.50.d_ref.refs_4_ = bf16[1152,1024]{1,0:T(8,128)(2,1)S(1)} custom-call(bf16[2048,256]{1,0:T(8,128)(2,1)S(1)} %bitcast.34), custom_call_target="tpu_custom_call" | custom-call | flops 450000000 | bytes 3407872 | tf_op jit(solution)/shard_map/pallas_call | solution.py:132
  16.1 3.4 %collective-permute-done.1.bot_ref.refs_6_ = bf16[128,256]{1,0:T(8,128)(2,1)S(1)} collective-permute-done((bf16[128,256]{1,0:T(8,128)(2,1)}, bf16[128,256]{1,0:T(8,128)(2,1)S(1)}, u32[]{:S(2)}, u32[]{:S(2)}) %collective-permute-start.1) | collective-permute-done | bytes 65568 | tf_op jit(solution)/shard_map/ppermute | solution.py:183
  19.5 2.4 %shard_map.52 = (f32[1152,128]{1,0:T(8,128)S(1)}, bf16[256,1024]{1,0:T(8,128)(2,1)S(1)}, bf16[768,128]{1,0:T(8,128)(2,1)S(1)}) custom-call(s32[1]{0:T(128)} %bitcast.11.core_ref, s32[1]{0:T(128)} %bitcast.slab_ref, bf16[512,128]{1,0:T(8,128)(2,1)S(1)} %bitcast.41, bf16[512,128]{1,0:T(8,128)(2,1)} %bitcast.14.refs_1_, bf16[512,128]{1,0:T(8,128)(2,1)} %bitcast.15.refs_2_, ...), custom_call_target="tpu_custom_call" | custom-call | flops 300000000 | bytes 4325384 | tf_op jit(solution)/shard_map/pallas_call | solution.py:132
  22.0 0.9 %shard_map.53.keep_ref = f32[1152,128]{1,0:T(8,128)S(1)} custom-call(s32[1]{0:T(128)} %bitcast.11.core_ref, bf16[256,1024]{1,0:T(8,128)(2,1)S(1)} %get-tuple-element.21.m_ref, bf16[1152,1024]{1,0:T(8,128)(2,1)S(1)} %shard_map.50.d_ref.refs_4_, bf16[768,128]{1,0:T(8,128)(2,1)S(1)} %get-tuple-element.22.edge_ref), custom_call_target="tpu_custom_call" | custom-call | flops 300000000 | bytes 3670020 | tf_op jit(solution)/shard_map/pallas_call | solution.py:132
  22.8 1.1 %collective-permute-done.8.came_ref = f32[1152,128]{1,0:T(8,128)S(1)} collective-permute-done((f32[1152,128]{1,0:T(8,128)S(1)}, f32[1152,128]{1,0:T(8,128)S(1)}, u32[]{:S(2)}, u32[]{:S(2)}) %collective-permute-start.8) | collective-permute-done | bytes 589856 | tf_op jit(solution)/shard_map/ppermute | solution.py:200
  24.0 14.3 %all_to_all.15 = bf16[16,72,128]{2,1,0:T(8,128)(2,1)S(1)} all-to-all(bf16[16,72,128]{2,1,0:T(8,128)(2,1)S(1)} %bitcast.38), channel_id=1, replica_groups=mesh['zh'=2,'x'=4,'y'=4,'c'=2,'s'=4] {'x','y'}, dimensions={0} | all-to-all | bytes 589824 | tf_op jit(solution)/shard_map/all_to_all | solution.py:162
  38.3 20.0 %all_to_all.16 = f32[8,72,128]{2,1,0:T(8,128)S(1)} all-to-all(f32[8,72,128]{2,1,0:T(8,128)S(1)} %bitcast.36), channel_id=1, replica_groups=mesh['zh'=2,'x'=4,'y'=4,'c'=2,'s'=4] {'zh','s'}, dimensions={0} | all-to-all | bytes 589824 | tf_op jit(solution)/shard_map/all_to_all | solution.py:162
  58.3 0.7 shard_map.56
  59.0 5.7 %all-to-all-start.2 = ((bf16[16,72,128]{2,1,0:T(8,128)(2,1)}), bf16[16,72,128]{2,1,0:T(8,128)(2,1)}, u32[]{:S(2)}, u32[]{:S(2)}) async-start(bf16[16,72,128]{2,1,0:T(8,128)(2,1)} %bitcast.21), calls=%async_computation.2 | async-start | bytes 589824 | tf_op jit(solution)/shard_map/all_to_all | solution.py:162
  64.7 1.9 %shard_map.51 = (bf16[512,128]{1,0:T(8,128)(2,1)S(1)}, bf16[512,128]{1,0:T(8,128)(2,1)}, bf16[512,128]{1,0:T(8,128)(2,1)S(1)}, bf16[512,128]{1,0:T(8,128)(2,1)S(1)}) custom-call(s32[1]{0:T(128)} %bitcast.slab_ref, bf16[9,256,128]{2,1,0:T(8,128)(2,1)S(1)} %bitcast.39, bf16[1152,1024]{1,0:T(8,128)(2,1)S(1)} %shard_map.50.d_ref.refs_4_, ...), custom_call_target="tpu_custom_call" | custom-call | flops 600000000 | bytes 3604484 | tf_op jit(solution)/shard_map/pallas_call | solution.py:132
  67.7 3.3 %collective-permute-start.4 = (bf16[512,128]{1,0:T(8,128)(2,1)S(1)}, bf16[512,128]{1,0:T(8,128)(2,1)S(1)}, u32[]{:S(2)}, u32[]{:S(2)}) collective-permute-start(bf16[512,128]{1,0:T(8,128)(2,1)S(1)} %get-tuple-element.16), channel_id=1, source_target_pairs={{0,3},{1,2},{2,1},{3,0},{4,7},{5,6},{6,5},{7,4},{8,11},{9,10},{10,... | collective-permute-start | bytes 393224 | tf_op jit(solution)/shard_map/ppermute | solution.py:158
  71.4 1.6 %collective-permute-done.2 = bf16[512,128]{1,0:T(8,128)(2,1)S(1)} collective-permute-done((bf16[512,128]{1,0:T(8,128)(2,1)}, bf16[512,128]{1,0:T(8,128)(2,1)S(1)}, u32[]{:S(2)}, u32[]{:S(2)}) %collective-permute-start.2) | collective-permute-done | bytes 131104 | tf_op jit(solution)/shard_map/ppermute | solution.py:158
  73.0 3.7 %collective-permute-done.3 = bf16[512,128]{1,0:T(8,128)(2,1)S(1)} collective-permute-done((bf16[512,128]{1,0:T(8,128)(2,1)S(1)}, bf16[512,128]{1,0:T(8,128)(2,1)S(1)}, u32[]{:S(2)}, u32[]{:S(2)}) %collective-permute-start.3) | collective-permute-done | bytes 131104 | tf_op jit(solution)/shard_map/ppermute | solution.py:158
  76.8 0.9 %copy_bitcast_fusion.1 = bf16[1,64,32,128]{3,2,1,0:T(8,128)(2,1)} fusion(bf16[64,1,8,128]{3,2,0,1:T(8,128)(2,1)S(1)} %get-tuple-element.29, bf16[64,1,8,128]{3,2,0,1:T(8,128)(2,1)S(1)} %get-tuple-element.30, bf16[64,1,8,128]{3,2,0,1:T(8,128)(2,1)S(1)} %get-tuple-element.31, bf16[64,1,8,128]{3,2,0,1:T(8,128)(2,1)S(1)} %get-tuple-element.28), kind=kLoop, calls=%fused_computation.3 | loop fusion | flops 786432 | bytes 1048576 | tf_op jit(solution)/shard_map/reshape | solution.py:221
  77.7 1.0 %broadcast_select_fusion.1 = (bf16[9,128,128]{2,1,0:T(8,128)(2,1)S(1)}, bf16[9,128,128]{2,1,0:T(8,128)(2,1)S(1)}) fusion(bf16[9,128,128]{2,1,0:T(8,128)(2,1)} %bitcast.22, bf16[9,128,128]{2,1,0:T(8,128)(2,1)S(1)} %collective-permute-done.9, pred[]{:T(512)S(6)} %eq.51), kind=kLoop, calls=%fused_computation.5 | loop fusion | flops 294912 | bytes 1179649 | tf_op jit(solution)/shard_map/jit(_where)/select_n | solution.py:210
  78.8 1.1 %maximum_convert_fusion = f32[3,3,256,128]{3,2,1,0:T(8,128)} fusion(bf16[3,3,128,128]{3,2,1,0:T(8,128)(2,1)S(1)} %bitcast.44, bf16[3,3,128,128]{3,2,1,0:T(8,128)(2,1)S(1)} %bitcast.43), kind=kLoop, calls=%fused_computation.1 | loop fusion | flops 1179648 | bytes 1769472 | tf_op jit(solution)/shard_map/convert_element_type | solution.py:222
  (24 shorter events, 2.4 us)
Async XLA Ops:
  0.6 1.0 %copy-start.2 = (bf16[1,64,32,128]{3,2,1,0:T(8,128)(2,1)S(1)}, bf16[1,64,32,128]{3,2,1,0:T(8,128)(2,1)}, u32[]{:S(2)}) copy-start(bf16[1,64,32,128]{3,2,1,0:T(8,128)(2,1)} %param.3) | copy-start | bytes 1572868
  2.6 0.7 copy-start.3
  3.2 16.3 %collective-permute-start.5 = (bf16[64,8,128]{2,1,0:T(8,128)(2,1)}, bf16[64,8,128]{2,1,0:T(8,128)(2,1)}, u32[]{:S(2)}, u32[]{:S(2)}) collective-permute-start(bf16[64,8,128]{2,1,0:T(8,128)(2,1)} %get-tuple-element.18), channel_id=1, source_target_pairs={{0,1},{1,0},{2,3},{3,2},{4,5},{5,4},{6,7},{7,6},{8,9},{9,8},{10,11... | collective-permute-start | bytes 393224 | tf_op jit(solution)/shard_map/ppermute | solution.py:158
  5.1 14.3 %collective-permute-start.6 = (bf16[64,8,128]{2,1,0:T(8,128)(2,1)}, bf16[64,8,128]{2,1,0:T(8,128)(2,1)}, u32[]{:S(2)}, u32[]{:S(2)}) collective-permute-start(bf16[64,8,128]{2,1,0:T(8,128)(2,1)} %get-tuple-element.19), channel_id=1, source_target_pairs={{0,2},{1,3},{2,0},{3,1},{4,6},{5,7},{6,4},{7,5},{8,10},{9,11},{10,... | collective-permute-start | bytes 393224 | tf_op jit(solution)/shard_map/ppermute | solution.py:158
  8.4 6.0 %copy-start = (bf16[1,128,16,256]{3,2,1,0:T(8,128)(2,1)S(1)}, bf16[1,128,16,256]{3,2,1,0:T(8,128)(2,1)}, u32[]{:S(2)}) copy-start(bf16[1,128,16,256]{3,2,1,0:T(8,128)(2,1)} %param.4) | copy-start | bytes 3145732
  8.4 11.1 %collective-permute-start.7 = (bf16[64,8,128]{2,1,0:T(8,128)(2,1)}, bf16[64,8,128]{2,1,0:T(8,128)(2,1)}, u32[]{:S(2)}, u32[]{:S(2)}) collective-permute-start(bf16[64,8,128]{2,1,0:T(8,128)(2,1)} %get-tuple-element.20), channel_id=1, source_target_pairs={{0,3},{1,2},{2,1},{3,0},{4,7},{5,6},{6,5},{7,4},{8,11},{9,10},{10,... | collective-permute-start | bytes 393224 | tf_op jit(solution)/shard_map/ppermute | solution.py:158
  10.7 5.4 %collective-permute-start = (bf16[128,256]{1,0:T(8,128)(2,1)}, bf16[128,256]{1,0:T(8,128)(2,1)S(1)}, u32[]{:S(2)}, u32[]{:S(2)}) collective-permute-start(bf16[128,256]{1,0:T(8,128)(2,1)} %get-tuple-element.25), channel_id=1, source_target_pairs={{0,1},{1,2},{2,3},{4,5},{5,6},{6,7},{8,9},{9,10},{10,11},{12,13},{... | collective-permute-start | bytes 196616 | tf_op jit(solution)/shard_map/ppermute | solution.py:182
  13.1 6.4 %collective-permute-start.1 = (bf16[128,256]{1,0:T(8,128)(2,1)}, bf16[128,256]{1,0:T(8,128)(2,1)S(1)}, u32[]{:S(2)}, u32[]{:S(2)}) collective-permute-start(bf16[128,256]{1,0:T(8,128)(2,1)} %get-tuple-element.24), channel_id=1, source_target_pairs={{1,0},{2,1},{3,2},{5,4},{6,5},{7,6},{9,8},{10,9},{11,10},{13,12},{... | collective-permute-start | bytes 196616 | tf_op jit(solution)/shard_map/ppermute | solution.py:183
  14.4 5.1 %copy-start.4 = (bf16[64,8,128]{2,1,0:T(8,128)(2,1)S(1)}, bf16[64,8,128]{2,1,0:T(8,128)(2,1)}, u32[]{:S(2)}) copy-start(bf16[64,8,128]{2,1,0:T(8,128)(2,1)} %copy-done.3) | copy-start | bytes 393220
  21.9 2.1 %collective-permute-start.8 = (f32[1152,128]{1,0:T(8,128)S(1)}, f32[1152,128]{1,0:T(8,128)S(1)}, u32[]{:S(2)}, u32[]{:S(2)}) collective-permute-start(f32[1152,128]{1,0:T(8,128)S(1)} %get-tuple-element.23), channel_id=1, source_target_pairs={{0,4},{4,0},{1,5},{5,1},{2,6},{6,2},{3,7},{7,3},{8,12},{12,8},{9,1... | collective-permute-start | bytes 1769480 | tf_op jit(solution)/shard_map/ppermute | solution.py:200
  38.3 26.5 %copy-start.1 = (bf16[3,3,256,128]{3,2,1,0:T(8,128)(2,1)S(1)}, bf16[3,3,256,128]{3,2,1,0:T(8,128)(2,1)}, u32[]{:S(2)}) copy-start(bf16[3,3,256,128]{3,2,1,0:T(8,128)(2,1)} %param.5) | copy-start | bytes 1769476
  59.0 12.4 %all-to-all-start.2 = ((bf16[16,72,128]{2,1,0:T(8,128)(2,1)}), bf16[16,72,128]{2,1,0:T(8,128)(2,1)}, u32[]{:S(2)}, u32[]{:S(2)}) async-start(bf16[16,72,128]{2,1,0:T(8,128)(2,1)} %bitcast.21), calls=%async_computation.2 | async-start | bytes 589824 | tf_op jit(solution)/shard_map/all_to_all | solution.py:162
  66.6 6.4 %collective-permute-start.2 = (bf16[512,128]{1,0:T(8,128)(2,1)}, bf16[512,128]{1,0:T(8,128)(2,1)S(1)}, u32[]{:S(2)}, u32[]{:S(2)}) collective-permute-start(bf16[512,128]{1,0:T(8,128)(2,1)} %get-tuple-element.14), channel_id=1, source_target_pairs={{0,1},{1,0},{2,3},{3,2},{4,5},{5,4},{6,7},{7,6},{8,9},{9,8},{10,11... | collective-permute-start | bytes 393224 | tf_op jit(solution)/shard_map/ppermute | solution.py:158
  67.2 9.6 %collective-permute-start.3 = (bf16[512,128]{1,0:T(8,128)(2,1)S(1)}, bf16[512,128]{1,0:T(8,128)(2,1)S(1)}, u32[]{:S(2)}, u32[]{:S(2)}) collective-permute-start(bf16[512,128]{1,0:T(8,128)(2,1)S(1)} %get-tuple-element.15), channel_id=1, source_target_pairs={{0,2},{1,3},{2,0},{3,1},{4,6},{5,7},{6,4},{7,5},{8,10},{9,11},{10,... | collective-permute-start | bytes 393224 | tf_op jit(solution)/shard_map/ppermute | solution.py:158
  67.7 9.0 %collective-permute-start.4 = (bf16[512,128]{1,0:T(8,128)(2,1)S(1)}, bf16[512,128]{1,0:T(8,128)(2,1)S(1)}, u32[]{:S(2)}, u32[]{:S(2)}) collective-permute-start(bf16[512,128]{1,0:T(8,128)(2,1)S(1)} %get-tuple-element.16), channel_id=1, source_target_pairs={{0,3},{1,2},{2,1},{3,0},{4,7},{5,6},{6,5},{7,4},{8,11},{9,10},{10,... | collective-permute-start | bytes 393224 | tf_op jit(solution)/shard_map/ppermute | solution.py:158
  71.4 6.3 %collective-permute-start.9 = (bf16[9,128,128]{2,1,0:T(8,128)(2,1)}, bf16[9,128,128]{2,1,0:T(8,128)(2,1)S(1)}, u32[]{:S(2)}, u32[]{:S(2)}) collective-permute-start(bf16[9,128,128]{2,1,0:T(8,128)(2,1)} %bitcast.22), channel_id=1, source_target_pairs={{0,4},{4,0},{1,5},{5,1},{2,6},{6,2},{3,7},{7,3},{8,12},{12,8},{9,1... | collective-permute-start | bytes 884744 | tf_op jit(solution)/shard_map/ppermute | solution.py:208

commit v3 on v2

--- a/solution.py
+++ b/solution.py
@@ -24,7 +24,18 @@
     return jnp.concatenate([wide[:, 128 * b : 128 * b + 128] for b in range(3)], axis=0)
 
 
-def pool_kernel(cot_ref, d_ref, y_ref):
+def ends_kernel(cot_ref, last_ref, first_ref):
+    line = lax.broadcasted_iota(jnp.int32, (32, 256), 0)
+    col = lax.broadcasted_iota(jnp.int32, (32, 256), 1)
+    want = jnp.where(line < 16, 16 * line + 15, 16 * (line - 16))
+    pick = jnp.where(col == want, 1.0, 0.0).astype(BF)
+    for i in range(8):
+        part = jnp.dot(pick, cot_ref[pl.ds(256 * i, 256), :], preferred_element_type=F32).astype(BF)
+        last_ref[pl.ds(16 * i, 16), :] = part[:16]
+        first_ref[pl.ds(16 * i, 16), :] = part[16:]
+
+
+def pool_kernel(cot_ref, d_ref, e_ref, y_ref):
     pick = picker()
     for i in range(8):
         part = jnp.dot(cot_ref[pl.ds(256 * i, 256), :], pick, preferred_element_type=F32)
@@ -36,17 +47,22 @@
             even = y_ref[b, pl.ds(2 * p, 128, stride=16), :]
             odd = y_ref[b, pl.ds(2 * p + 1, 128, stride=16), :]
             upper = even if above is None else above + even
-            d_ref[pl.ds(128 * (6 + b), 128), pl.ds(128 * p, 128)] = upper.astype(BF)
-            d_ref[pl.ds(128 * (3 + b), 128), pl.ds(128 * p, 128)] = (even + odd).astype(BF)
+            cells = [(6 + b, p, upper), (3 + b, p, even + odd)]
             if p > 0:
-                d_ref[pl.ds(128 * b, 128), pl.ds(128 * (p - 1), 128)] = upper.astype(BF)
+                cells.append((b, p - 1, upper))
+            if p == 7:
+                cells.append((b, 7, odd))
             above = odd
-        d_ref[pl.ds(128 * b, 128), pl.ds(896, 128)] = above.astype(BF)
-
-
-def products(pixels, d_ref, edge_ref, out_ref):
+            for k, q, value in cells:
+                high = value.astype(BF)
+                d_ref[pl.ds(128 * k, 128), pl.ds(128 * q, 128)] = high
+                e_ref[pl.ds(128 * k, 128), pl.ds(128 * q, 128)] = (value - high.astype(F32)).astype(BF)
+
+
+def products(pixels, d_ref, e_ref, edge_ref, out_ref):
     for k in range(0, 9, 3):
         part = lax.dot_general(pixels, d_ref[pl.ds(128 * k, 384), :], NT, preferred_element_type=F32)
+        part += lax.dot_general(pixels, e_ref[pl.ds(128 * k, 384), :], NT, preferred_element_type=F32)
         if k != 3:
             p = 7 if k == 0 else 0
             edge = edge_ref[pl.ds(64 * k, 384), :]
@@ -74,7 +90,7 @@
 
 
 def send_kernel(core_ref, slab_ref, *refs):
-    d_ref, top_ref, bot_ref, send_ref, m_ref, edge_ref, f_ref = refs[4:]
+    d_ref, e_ref, top_ref, bot_ref, send_ref, m_ref, edge_ref, f_ref = refs[4:]
     pick = picker()
     edge_ref[pl.ds(0, 384), :] = stacked(jnp.dot(bot_ref[...], pick, preferred_element_type=F32)).astype(BF)
     edge_ref[pl.ds(384, 384), :] = stacked(jnp.dot(top_ref[...], pick, preferred_element_type=F32)).astype(BF)
@@ -83,11 +99,11 @@
         f_ref[pl.ds(place, 512), :] = refs[k][...].astype(F32)
     for p in range(8):
         m_ref[:, pl.ds(128 * p, 128)] = f_ref[pl.ds(p, 256, stride=8), :].astype(BF)
-    products(rows_of(m_ref, 1 - core_ref[0]), d_ref, edge_ref, send_ref)
-
-
-def keep_kernel(core_ref, m_ref, d_ref, edge_ref, keep_ref):
-    products(rows_of(m_ref, core_ref[0]), d_ref, edge_ref, keep_ref)
+    products(rows_of(m_ref, 1 - core_ref[0]), d_ref, e_ref, edge_ref, send_ref)
+
+
+def keep_kernel(core_ref, m_ref, d_ref, e_ref, edge_ref, keep_ref):
+    products(rows_of(m_ref, core_ref[0]), d_ref, e_ref, edge_ref, keep_ref)
 
 
 def join_kernel(keep_ref, came_ref, half_ref):
@@ -176,20 +192,22 @@
         compiler_params=pltpu.CompilerParams(vmem_limit_bytes=8 << 20),
         cost_estimate=pl.CostEstimate(flops=0, bytes_accessed=1048576, transcendentals=0),
         name="parted",
-    )(slab, images[0])
+    )(slab, pltpu.with_memory_space_constraint(images[0], pltpu.HBM))
     img = {k: swapped(blocks[k], k) for k in (3, 2, 1)}
     img = [x.reshape(512, 128) for x in (blocks[0], img[1], img[2], img[3])]
-    top = lax.ppermute(cot[:, 15, :], "s", DOWN)
-    bot = lax.ppermute(cot[:, 0, :], "s", UP)
-    (d,) = call(
-        pool_kernel, [S((1152, 1024), BF)],
+    rows_in = cot.reshape(2048, 256)
+    last, first = call(ends_kernel, [S((128, 256), BF)] * 2, [], 34000000, 0, rows_in)
+    top = lax.ppermute(last, "s", DOWN)
+    bot = lax.ppermute(first, "s", UP)
+    d, e = call(
+        pool_kernel, [S((1152, 1024), BF)] * 2,
         [pltpu.VMEM((3, 2048, 128), F32)], 450000000, 0, cot.reshape(2048, 256),
     )
     send, pixels, edges = call(
         send_kernel, [S((1152, 128), F32), S((256, 1024), BF), S((768, 128), BF)],
-        [pltpu.VMEM((2048, 128), F32)], 300000000, 2, core, slab, *img, d, top, bot,
-    )
-    (keep,) = call(keep_kernel, [S((1152, 128), F32)], [], 300000000, 1, core, pixels, d, edges)
+        [pltpu.VMEM((2048, 128), F32)], 300000000, 2, core, slab, *img, d, e, top, bot,
+    )
+    (keep,) = call(keep_kernel, [S((1152, 128), F32)], [], 300000000, 1, core, pixels, d, e, edges)
     low = call(
         image_kernel, [S((512, 128), BF)] * 4, [pltpu.VMEM((2048, 128), F32)],
         600000000, 1, slab, kernel.reshape(9, 256, 128), d, top, bot,
@@ -200,7 +218,7 @@
     came = lax.ppermute(send, "c", SWAP)
     (half,) = call(join_kernel, [S((1152, 128), BF)], [], 150000, 0, keep, came)
     half = exchange(half.reshape(across, rows, 128), ("x", "y"))
-    part = fold(half, along, F32)
+    part = fold(half, along, BF)
     part = exchange(part, ("zh", "s"))
     part = fold(part, across, BF)
     mine = exchange(part, ("x", "y"))

time: 80.4 us -> 76.7 us (0.954)
  blocking collectives: 34.2 us -> 31.8 us
  waiting for transfers between devices: 10.2 us -> 8.5 us
  local copies, waits for them, and re-layouts: 4 us -> 2.45 us
  Pallas kernels: 8.53 us -> 9.87 us
    all_to_all x2, blocking collectives: 34.2 us -> 31.8 us  [exchange(): return lax.all_to_all(x, axes, split_axis=0, concat_axis=0, tiled=True)]
    ppermute x2, waiting for transfers between devices: 3.36 us -> 2.06 us  [the longest x1 2.06 us: body(): bot = lax.ppermute(first, 's', UP)]
    pallas_call x7 -> x8, Pallas kernels: 7.66 us -> 8.72 us  [call(): pl.pallas_call(kernel, out_shape=tuple(outs), in_specs=ins, out_specs=tup...]
    unnamed x11 -> x6, local copies, waits for them, and re-layouts: 3.34 us -> 2.45 us
  transfers between devices with their start and end apart: 11 -> 11, of which waited for: 5 -> 5; matrix products, arithmetic and copies ran while one was open for 4% -> 1% of each run, Pallas kernels for 6% -> 8%
where the time goes in v3:
time: 76.7 us; the launch traced here: 76.2 us
  blocking collectives  31.8 us (41%)
  starting transfers between devices  19.7 us (26%)
  Pallas kernels  9.87 us (13%)
  waiting for transfers between devices  8.5 us (11%)
  other arithmetic  3.1 us (4%)
  local copies, waits for them, and re-layouts  2.45 us (3%)
    all_to_all x2, blocking collectives, exchange(): return lax.all_to_all(x, axes, split_axis=0, concat_axis=0, tiled=True)  31.8 us
    ppermute x6, starting transfers between devices, swapped(): return lax.ppermute(x, 's', [(i, i ^ k) for i in range(4)])  9.66 us
    pallas_call x8, Pallas kernels, call(): pl.pallas_call(kernel, out_shape=tuple(outs), in_specs=ins, out_specs=tup...  8.72 us
    all_to_all x1, starting transfers between devices, exchange(): return lax.all_to_all(x, axes, split_axis=0, concat_axis=0, tiled=True)  6.19 us
    ppermute x6, waiting for transfers between devices, swapped(): return lax.ppermute(x, 's', [(i, i ^ k) for i in range(4)])  5.63 us
    ppermute x1, starting transfers between devices, body(): top = lax.ppermute(last, 's', DOWN)  2.47 us
    unnamed x6, local copies, waits for them, and re-layouts  2.45 us
    ppermute x1, waiting for transfers between devices, body(): bot = lax.ppermute(first, 's', UP)  2.06 us
  transfers between devices with their start and end apart: 11, of which 5 were waited for; matrix products, arithmetic and copies ran while one was open for 1% of the time, Pallas kernels for 8%

profile of v3, /device:TPU:6, one launch (start us, length us, event | category | flops | bytes accessed | tf_op | source)
XLA Modules:
  0.0 76.2 jit_solution(13329817956669566188)
XLA Ops:
  0.6 1.1 %parted.1 = (bf16[64,8,128]{2,1,0:T(8,128)(2,1)S(1)}, bf16[64,8,128]{2,1,0:T(8,128)(2,1)S(1)}, bf16[64,8,128]{2,1,0:T(8,128)(2,1)S(1)}, bf16[64,8,128]{2,1,0:T(8,128)(2,1)S(1)}) custom-call(s32[1]{0:T(128)} %bitcast.slab_ref, bf16[64,32,128]{2,1,0:T(8,128)(2,1)} %bitcast.40), custom_call_target="tpu_custom_call" | custom-call | bytes 1048576 | tf_op jit(solution)/shard_map/parted/pallas_call | solution.py:186
  1.8 2.0 %collective-permute-start.5 = (bf16[64,8,128]{2,1,0:T(8,128)(2,1)S(1)}, bf16[64,8,128]{2,1,0:T(8,128)(2,1)S(1)}, u32[]{:S(2)}, u32[]{:S(2)}) collective-permute-start(bf16[64,8,128]{2,1,0:T(8,128)(2,1)S(1)} %get-tuple-element.25), channel_id=1, source_target_pairs={{0,1},{1,0},{2,3},{3,2},{4,5},{5,4},{6,7},{7,6},{8,9},{9,8},{10,11... | collective-permute-start | bytes 393224 | tf_op jit(solution)/shard_map/ppermute | solution.py:174
  3.8 3.3 %collective-permute-start.6 = (bf16[64,8,128]{2,1,0:T(8,128)(2,1)S(1)}, bf16[64,8,128]{2,1,0:T(8,128)(2,1)S(1)}, u32[]{:S(2)}, u32[]{:S(2)}) collective-permute-start(bf16[64,8,128]{2,1,0:T(8,128)(2,1)S(1)} %get-tuple-element.26), channel_id=1, source_target_pairs={{0,2},{1,3},{2,0},{3,1},{4,6},{5,7},{6,4},{7,5},{8,10},{9,11},{10,... | collective-permute-start | bytes 393224 | tf_op jit(solution)/shard_map/ppermute | solution.py:174
  7.1 1.2 %copy-done = bf16[1,128,16,256]{3,2,1,0:T(8,128)(2,1)S(1)} copy-done((bf16[1,128,16,256]{3,2,1,0:T(8,128)(2,1)S(1)}, bf16[1,128,16,256]{3,2,1,0:T(8,128)(2,1)}, u32[]{:S(2)}) %copy-start) | copy-done | bytes 1048600
  8.6 2.5 %collective-permute-start = (bf16[128,256]{1,0:T(8,128)(2,1)S(1)}, bf16[128,256]{1,0:T(8,128)(2,1)S(1)}, u32[]{:S(2)}, u32[]{:S(2)}) collective-permute-start(bf16[128,256]{1,0:T(8,128)(2,1)S(1)} %get-tuple-element.18), channel_id=1, source_target_pairs={{0,1},{1,2},{2,3},{4,5},{5,6},{6,7},{8,9},{9,10},{10,11},{12,13},{... | collective-permute-start | bytes 196616 | tf_op jit(solution)/shard_map/ppermute | solution.py:200
  11.0 1.3 %collective-permute-start.1 = (bf16[128,256]{1,0:T(8,128)(2,1)S(1)}, bf16[128,256]{1,0:T(8,128)(2,1)S(1)}, u32[]{:S(2)}, u32[]{:S(2)}) collective-permute-start(bf16[128,256]{1,0:T(8,128)(2,1)S(1)} %get-tuple-element.19), channel_id=1, source_target_pairs={{1,0},{2,1},{3,2},{5,4},{6,5},{7,6},{9,8},{10,9},{11,10},{13,12},{... | collective-permute-start | bytes 196616 | tf_op jit(solution)/shard_map/ppermute | solution.py:201
  12.4 1.2 %copy-done.1 = bf16[1,128,16,256]{3,2,1,0:T(8,128)(2,1)S(1)} copy-done((bf16[1,128,16,256]{3,2,1,0:T(8,128)(2,1)S(1)}, bf16[1,128,16,256]{3,2,1,0:T(8,128)(2,1)}, u32[]{:S(2)}) %copy-start.1) | copy-done | bytes 1048600
  13.6 2.1 %shard_map.50 = (bf16[1152,1024]{1,0:T(8,128)(2,1)S(1)}, bf16[1152,1024]{1,0:T(8,128)(2,1)S(1)}) custom-call(bf16[2048,256]{1,0:T(8,128)(2,1)S(1)} %bitcast.30), custom_call_target="tpu_custom_call" | custom-call | flops 450000000 | bytes 5767168 | tf_op jit(solution)/shard_map/pallas_call | solution.py:148
  15.7 2.1 %collective-permute-done.1.bot_ref.refs_7_ = bf16[128,256]{1,0:T(8,128)(2,1)S(1)} collective-permute-done((bf16[128,256]{1,0:T(8,128)(2,1)S(1)}, bf16[128,256]{1,0:T(8,128)(2,1)S(1)}, u32[]{:S(2)}, u32[]{:S(2)}) %collective-permute-start.1) | collective-permute-done | bytes 65568 | tf_op jit(solution)/shard_map/ppermute | solution.py:201
  17.8 2.0 %shard_map.53 = (f32[1152,128]{1,0:T(8,128)S(1)}, bf16[256,1024]{1,0:T(8,128)(2,1)S(1)}, bf16[768,128]{1,0:T(8,128)(2,1)S(1)}) custom-call(s32[1]{0:T(128)} %bitcast.8.core_ref, s32[1]{0:T(128)} %bitcast.slab_ref, bf16[512,128]{1,0:T(8,128)(2,1)S(1)} %bitcast.34, bf16[512,128]{1,0:T(8,128)(2,1)S(1)} %bitcast.35, bf16[512,128]{1,0:T(8,128)(2,1)S(1)} %bitcast.36, ...), custom_call_target="tpu_custom_call" | custom-call | flops 300000000 | bytes 6684680 | tf_op jit(solution)/shard_map/pallas_call | solution.py:148
  19.9 1.6 %shard_map.54.keep_ref = f32[1152,128]{1,0:T(8,128)S(1)} custom-call(s32[1]{0:T(128)} %bitcast.8.core_ref, bf16[256,1024]{1,0:T(8,128)(2,1)S(1)} %get-tuple-element.29.m_ref, bf16[1152,1024]{1,0:T(8,128)(2,1)S(1)} %get-tuple-element.17.d_ref.refs_4_, bf16[1152,1024]{1,0:T(8,128)(2,1)S(1)} %get-tuple-element.28.refs_5_.e_ref, ...), custom_call_target="tpu_custom_call" | custom-call | flops 300000000 | bytes 6029316 | tf_op jit(solution)/shard_map/pallas_call | solution.py:148
  22.0 14.4 %all_to_all.15 = bf16[16,72,128]{2,1,0:T(8,128)(2,1)S(1)} all-to-all(bf16[16,72,128]{2,1,0:T(8,128)(2,1)S(1)} %bitcast.28), channel_id=1, replica_groups=mesh['zh'=2,'x'=4,'y'=4,'c'=2,'s'=4] {'x','y'}, dimensions={0} | all-to-all | bytes 589824 | tf_op jit(solution)/shard_map/all_to_all | solution.py:178
  36.4 17.4 %all_to_all.16 = bf16[8,72,128]{2,1,0:T(8,128)(2,1)S(1)} all-to-all(bf16[8,72,128]{2,1,0:T(8,128)(2,1)S(1)} %bitcast.32), channel_id=1, replica_groups=mesh['zh'=2,'x'=4,'y'=4,'c'=2,'s'=4] {'zh','s'}, dimensions={0} | all-to-all | bytes 294912 | tf_op jit(solution)/shard_map/all_to_all | solution.py:178
  53.8 0.7 shard_map.57
  54.6 6.2 %all-to-all-start.2 = ((bf16[16,72,128]{2,1,0:T(8,128)(2,1)}), bf16[16,72,128]{2,1,0:T(8,128)(2,1)}, u32[]{:S(2)}, u32[]{:S(2)}) async-start(bf16[16,72,128]{2,1,0:T(8,128)(2,1)} %bitcast.18), calls=%async_computation.2 | async-start | bytes 589824 | tf_op jit(solution)/shard_map/all_to_all | solution.py:178
  60.8 1.9 %shard_map.52 = (bf16[512,128]{1,0:T(8,128)(2,1)S(1)}, bf16[512,128]{1,0:T(8,128)(2,1)}, bf16[512,128]{1,0:T(8,128)(2,1)S(1)}, bf16[512,128]{1,0:T(8,128)(2,1)S(1)}) custom-call(s32[1]{0:T(128)} %bitcast.slab_ref, bf16[9,256,128]{2,1,0:T(8,128)(2,1)S(1)} %bitcast.31, bf16[1152,1024]{1,0:T(8,128)(2,1)S(1)} %get-tuple-element.17.d_ref.refs_4_, ...), custom_call_target="tpu_custom_call" | custom-call | flops 600000000 | bytes 3604484 | tf_op jit(solution)/shard_map/pallas_call | solution.py:148
  62.7 0.6 collective-permute-start.2
  63.2 0.5 collective-permute-start.3
  63.7 3.4 %collective-permute-start.4 = (bf16[512,128]{1,0:T(8,128)(2,1)S(1)}, bf16[512,128]{1,0:T(8,128)(2,1)S(1)}, u32[]{:S(2)}, u32[]{:S(2)}) collective-permute-start(bf16[512,128]{1,0:T(8,128)(2,1)S(1)} %get-tuple-element.23), channel_id=1, source_target_pairs={{0,3},{1,2},{2,1},{3,0},{4,7},{5,6},{6,5},{7,4},{8,11},{9,10},{10,... | collective-permute-start | bytes 393224 | tf_op jit(solution)/shard_map/ppermute | solution.py:174
  67.5 1.9 %collective-permute-done.2 = bf16[512,128]{1,0:T(8,128)(2,1)S(1)} collective-permute-done((bf16[512,128]{1,0:T(8,128)(2,1)}, bf16[512,128]{1,0:T(8,128)(2,1)S(1)}, u32[]{:S(2)}, u32[]{:S(2)}) %collective-permute-start.2) | collective-permute-done | bytes 131104 | tf_op jit(solution)/shard_map/ppermute | solution.py:174
  69.3 3.8 %collective-permute-done.3 = bf16[512,128]{1,0:T(8,128)(2,1)S(1)} collective-permute-done((bf16[512,128]{1,0:T(8,128)(2,1)S(1)}, bf16[512,128]{1,0:T(8,128)(2,1)S(1)}, u32[]{:S(2)}, u32[]{:S(2)}) %collective-permute-start.3) | collective-permute-done | bytes 131104 | tf_op jit(solution)/shard_map/ppermute | solution.py:174
  73.1 0.9 %copy_bitcast_fusion = bf16[1,64,32,128]{3,2,1,0:T(8,128)(2,1)} fusion(bf16[64,1,8,128]{3,2,0,1:T(8,128)(2,1)S(1)} %get-tuple-element.35, bf16[64,1,8,128]{3,2,0,1:T(8,128)(2,1)S(1)} %get-tuple-element.36, bf16[64,1,8,128]{3,2,0,1:T(8,128)(2,1)S(1)} %get-tuple-element.37, bf16[64,1,8,128]{3,2,0,1:T(8,128)(2,1)S(1)} %get-tuple-element.34), kind=kLoop, calls=%fused_computation.2 | loop fusion | flops 786432 | bytes 1048576 | tf_op jit(solution)/shard_map/reshape | solution.py:239
  74.0 1.0 %broadcast_select_fusion.1 = (bf16[9,128,128]{2,1,0:T(8,128)(2,1)S(1)}, bf16[9,128,128]{2,1,0:T(8,128)(2,1)S(1)}) fusion(bf16[9,128,128]{2,1,0:T(8,128)(2,1)} %bitcast.19, bf16[9,128,128]{2,1,0:T(8,128)(2,1)S(1)} %collective-permute-done.9, pred[]{:T(512)S(6)} %eq.51), kind=kLoop, calls=%fused_computation.4 | loop fusion | flops 294912 | bytes 1179649 | tf_op jit(solution)/shard_map/jit(_where)/select_n | solution.py:228
  75.1 1.1 %maximum_convert_fusion = f32[3,3,256,128]{3,2,1,0:T(8,128)} fusion(bf16[3,3,128,128]{3,2,1,0:T(8,128)(2,1)S(1)} %bitcast.39, bf16[3,3,128,128]{3,2,1,0:T(8,128)(2,1)S(1)} %bitcast.38), kind=kLoop, calls=%fused_computation | loop fusion | flops 1179648 | bytes 1769472 | tf_op jit(solution)/shard_map/convert_element_type | solution.py:240
  (19 shorter events, 1.4 us)
Async XLA Ops:
  1.8 16.0 %collective-permute-start.5 = (bf16[64,8,128]{2,1,0:T(8,128)(2,1)S(1)}, bf16[64,8,128]{2,1,0:T(8,128)(2,1)S(1)}, u32[]{:S(2)}, u32[]{:S(2)}) collective-permute-start(bf16[64,8,128]{2,1,0:T(8,128)(2,1)S(1)} %get-tuple-element.25), channel_id=1, source_target_pairs={{0,1},{1,0},{2,3},{3,2},{4,5},{5,4},{6,7},{7,6},{8,9},{9,8},{10,11... | collective-permute-start | bytes 393224 | tf_op jit(solution)/shard_map/ppermute | solution.py:174
  3.8 14.0 %collective-permute-start.6 = (bf16[64,8,128]{2,1,0:T(8,128)(2,1)S(1)}, bf16[64,8,128]{2,1,0:T(8,128)(2,1)S(1)}, u32[]{:S(2)}, u32[]{:S(2)}) collective-permute-start(bf16[64,8,128]{2,1,0:T(8,128)(2,1)S(1)} %get-tuple-element.26), channel_id=1, source_target_pairs={{0,2},{1,3},{2,0},{3,1},{4,6},{5,7},{6,4},{7,5},{8,10},{9,11},{10,... | collective-permute-start | bytes 393224 | tf_op jit(solution)/shard_map/ppermute | solution.py:174
  7.1 10.7 %collective-permute-start.7 = (bf16[64,8,128]{2,1,0:T(8,128)(2,1)S(1)}, bf16[64,8,128]{2,1,0:T(8,128)(2,1)S(1)}, u32[]{:S(2)}, u32[]{:S(2)}) collective-permute-start(bf16[64,8,128]{2,1,0:T(8,128)(2,1)S(1)} %get-tuple-element.27), channel_id=1, source_target_pairs={{0,3},{1,2},{2,1},{3,0},{4,7},{5,6},{6,5},{7,4},{8,11},{9,10},{10,... | collective-permute-start | bytes 393224 | tf_op jit(solution)/shard_map/ppermute | solution.py:174
  7.1 1.2 %copy-start = (bf16[1,128,16,256]{3,2,1,0:T(8,128)(2,1)S(1)}, bf16[1,128,16,256]{3,2,1,0:T(8,128)(2,1)}, u32[]{:S(2)}) copy-start(bf16[1,128,16,256]{3,2,1,0:T(8,128)(2,1)} %param.4) | copy-start | bytes 3145732
  8.6 7.1 %collective-permute-start = (bf16[128,256]{1,0:T(8,128)(2,1)S(1)}, bf16[128,256]{1,0:T(8,128)(2,1)S(1)}, u32[]{:S(2)}, u32[]{:S(2)}) collective-permute-start(bf16[128,256]{1,0:T(8,128)(2,1)S(1)} %get-tuple-element.18), channel_id=1, source_target_pairs={{0,1},{1,2},{2,3},{4,5},{5,6},{6,7},{8,9},{9,10},{10,11},{12,13},{... | collective-permute-start | bytes 196616 | tf_op jit(solution)/shard_map/ppermute | solution.py:200
  11.0 6.7 %collective-permute-start.1 = (bf16[128,256]{1,0:T(8,128)(2,1)S(1)}, bf16[128,256]{1,0:T(8,128)(2,1)S(1)}, u32[]{:S(2)}, u32[]{:S(2)}) collective-permute-start(bf16[128,256]{1,0:T(8,128)(2,1)S(1)} %get-tuple-element.19), channel_id=1, source_target_pairs={{1,0},{2,1},{3,2},{5,4},{6,5},{7,6},{9,8},{10,9},{11,10},{13,12},{... | collective-permute-start | bytes 196616 | tf_op jit(solution)/shard_map/ppermute | solution.py:201
  12.4 1.2 %copy-start.1 = (bf16[1,128,16,256]{3,2,1,0:T(8,128)(2,1)S(1)}, bf16[1,128,16,256]{3,2,1,0:T(8,128)(2,1)}, u32[]{:S(2)}) copy-start(bf16[1,128,16,256]{3,2,1,0:T(8,128)(2,1)} %param.4) | copy-start | bytes 3145732
  19.8 2.1 %collective-permute-start.8 = (f32[1152,128]{1,0:T(8,128)S(1)}, f32[1152,128]{1,0:T(8,128)S(1)}, u32[]{:S(2)}, u32[]{:S(2)}) collective-permute-start(f32[1152,128]{1,0:T(8,128)S(1)} %get-tuple-element.31), channel_id=1, source_target_pairs={{0,4},{4,0},{1,5},{5,1},{2,6},{6,2},{3,7},{7,3},{8,12},{12,8},{9,1... | collective-permute-start | bytes 1769480 | tf_op jit(solution)/shard_map/ppermute | solution.py:218
  21.9 38.8 %copy-start.2 = (bf16[3,3,256,128]{3,2,1,0:T(8,128)(2,1)S(1)}, bf16[3,3,256,128]{3,2,1,0:T(8,128)(2,1)}, u32[]{:S(2)}) copy-start(bf16[3,3,256,128]{3,2,1,0:T(8,128)(2,1)} %param.5) | copy-start | bytes 1769476
  54.6 12.9 %all-to-all-start.2 = ((bf16[16,72,128]{2,1,0:T(8,128)(2,1)}), bf16[16,72,128]{2,1,0:T(8,128)(2,1)}, u32[]{:S(2)}, u32[]{:S(2)}) async-start(bf16[16,72,128]{2,1,0:T(8,128)(2,1)} %bitcast.18), calls=%async_computation.2 | async-start | bytes 589824 | tf_op jit(solution)/shard_map/all_to_all | solution.py:178
  62.7 6.6 %collective-permute-start.2 = (bf16[512,128]{1,0:T(8,128)(2,1)}, bf16[512,128]{1,0:T(8,128)(2,1)S(1)}, u32[]{:S(2)}, u32[]{:S(2)}) collective-permute-start(bf16[512,128]{1,0:T(8,128)(2,1)} %get-tuple-element.21), channel_id=1, source_target_pairs={{0,1},{1,0},{2,3},{3,2},{4,5},{5,4},{6,7},{7,6},{8,9},{9,8},{10,11... | collective-permute-start | bytes 393224 | tf_op jit(solution)/shard_map/ppermute | solution.py:174
  63.2 9.8 %collective-permute-start.3 = (bf16[512,128]{1,0:T(8,128)(2,1)S(1)}, bf16[512,128]{1,0:T(8,128)(2,1)S(1)}, u32[]{:S(2)}, u32[]{:S(2)}) collective-permute-start(bf16[512,128]{1,0:T(8,128)(2,1)S(1)} %get-tuple-element.22), channel_id=1, source_target_pairs={{0,2},{1,3},{2,0},{3,1},{4,6},{5,7},{6,4},{7,5},{8,10},{9,11},{10,... | collective-permute-start | bytes 393224 | tf_op jit(solution)/shard_map/ppermute | solution.py:174
  63.7 9.4 %collective-permute-start.4 = (bf16[512,128]{1,0:T(8,128)(2,1)S(1)}, bf16[512,128]{1,0:T(8,128)(2,1)S(1)}, u32[]{:S(2)}, u32[]{:S(2)}) collective-permute-start(bf16[512,128]{1,0:T(8,128)(2,1)S(1)} %get-tuple-element.23), channel_id=1, source_target_pairs={{0,3},{1,2},{2,1},{3,0},{4,7},{5,6},{6,5},{7,4},{8,11},{9,10},{10,... | collective-permute-start | bytes 393224 | tf_op jit(solution)/shard_map/ppermute | solution.py:174
  67.5 6.6 %collective-permute-start.9 = (bf16[9,128,128]{2,1,0:T(8,128)(2,1)}, bf16[9,128,128]{2,1,0:T(8,128)(2,1)S(1)}, u32[]{:S(2)}, u32[]{:S(2)}) collective-permute-start(bf16[9,128,128]{2,1,0:T(8,128)(2,1)} %bitcast.19), channel_id=1, source_target_pairs={{0,4},{4,0},{1,5},{5,1},{2,6},{6,2},{3,7},{7,3},{8,12},{12,8},{9,1... | collective-permute-start | bytes 884744 | tf_op jit(solution)/shard_map/ppermute | solution.py:226

commit v4 on v3

--- a/solution.py
+++ b/solution.py
@@ -60,16 +60,16 @@
 
 
 def products(pixels, d_ref, e_ref, edge_ref, out_ref):
-    for k in range(0, 9, 3):
-        part = lax.dot_general(pixels, d_ref[pl.ds(128 * k, 384), :], NT, preferred_element_type=F32)
-        part += lax.dot_general(pixels, e_ref[pl.ds(128 * k, 384), :], NT, preferred_element_type=F32)
-        if k != 3:
-            p = 7 if k == 0 else 0
-            edge = edge_ref[pl.ds(64 * k, 384), :]
+    for k, count, edge, p in ((0, 2, 0, 7), (2, 1, 2, 7), (3, 2, None, 0), (5, 1, None, 0), (6, 2, 3, 0), (8, 1, 5, 0)):
+        span = pl.ds(128 * k, 128 * count)
+        part = lax.dot_general(pixels, d_ref[span, :], NT, preferred_element_type=F32)
+        part += lax.dot_general(pixels, e_ref[span, :], NT, preferred_element_type=F32)
+        if edge is not None:
             part += lax.dot_general(
-                pixels[:, 128 * p : 128 * p + 128], edge, NT, preferred_element_type=F32
+                pixels[:, 128 * p : 128 * p + 128], edge_ref[pl.ds(128 * edge, 128 * count), :], NT,
+                preferred_element_type=F32,
             )
-        for u in range(3):
+        for u in range(count):
             out_ref[pl.ds(128 * (k + u), 128), :] = part[:, 128 * u : 128 * u + 128]
 
 
@@ -193,7 +193,9 @@
         cost_estimate=pl.CostEstimate(flops=0, bytes_accessed=1048576, transcendentals=0),
         name="parted",
     )(slab, pltpu.with_memory_space_constraint(images[0], pltpu.HBM))
-    img = {k: swapped(blocks[k], k) for k in (3, 2, 1)}
+    img = {}
+    for k in (3, 2, 1):
+        img[k] = swapped(blocks[k], k)
     img = [x.reshape(512, 128) for x in (blocks[0], img[1], img[2], img[3])]
     rows_in = cot.reshape(2048, 256)
     last, first = call(ends_kernel, [S((128, 256), BF)] * 2, [], 34000000, 0, rows_in)

time: 76.7 us -> 76.7 us (level)
  no operation moved by 1% of the time
where the time goes in v4:
time: 76.7 us; the launch traced here: 76.2 us
  blocking collectives  31.8 us (41%)
  starting transfers between devices  19.7 us (26%)
  Pallas kernels  9.87 us (13%)
  waiting for transfers between devices  8.5 us (11%)
  other arithmetic  3.1 us (4%)
  local copies, waits for them, and re-layouts  2.45 us (3%)
    all_to_all x2, blocking collectives, exchange(): return lax.all_to_all(x, axes, split_axis=0, concat_axis=0, tiled=True)  31.8 us
    ppermute x6, starting transfers between devices, swapped(): return lax.ppermute(x, 's', [(i, i ^ k) for i in range(4)])  9.66 us
    pallas_call x8, Pallas kernels, call(): pl.pallas_call(kernel, out_shape=tuple(outs), in_specs=ins, out_specs=tup...  8.72 us
    all_to_all x1, starting transfers between devices, exchange(): return lax.all_to_all(x, axes, split_axis=0, concat_axis=0, tiled=True)  6.19 us
    ppermute x6, waiting for transfers between devices, swapped(): return lax.ppermute(x, 's', [(i, i ^ k) for i in range(4)])  5.63 us
    ppermute x1, starting transfers between devices, body(): top = lax.ppermute(last, 's', DOWN)  2.47 us
    unnamed x6, local copies, waits for them, and re-layouts  2.45 us
    ppermute x1, waiting for transfers between devices, body(): bot = lax.ppermute(first, 's', UP)  2.06 us
  transfers between devices with their start and end apart: 11, of which 5 were waited for; matrix products, arithmetic and copies ran while one was open for 1% of the time, Pallas kernels for 8%

profile of v4, /device:TPU:6, one launch (start us, length us, event | category | flops | bytes accessed | tf_op | source)
XLA Modules:
  0.0 76.2 jit_solution(13005308168442438868)
XLA Ops:
  0.6 1.1 %parted.1 = (bf16[64,8,128]{2,1,0:T(8,128)(2,1)S(1)}, bf16[64,8,128]{2,1,0:T(8,128)(2,1)S(1)}, bf16[64,8,128]{2,1,0:T(8,128)(2,1)S(1)}, bf16[64,8,128]{2,1,0:T(8,128)(2,1)S(1)}) custom-call(s32[1]{0:T(128)} %bitcast.slab_ref, bf16[64,32,128]{2,1,0:T(8,128)(2,1)} %bitcast.40), custom_call_target="tpu_custom_call" | custom-call | bytes 1048576 | tf_op jit(solution)/shard_map/parted/pallas_call | solution.py:186
  1.8 2.0 %collective-permute-start.5 = (bf16[64,8,128]{2,1,0:T(8,128)(2,1)S(1)}, bf16[64,8,128]{2,1,0:T(8,128)(2,1)S(1)}, u32[]{:S(2)}, u32[]{:S(2)}) collective-permute-start(bf16[64,8,128]{2,1,0:T(8,128)(2,1)S(1)} %get-tuple-element.25), channel_id=1, source_target_pairs={{0,1},{1,0},{2,3},{3,2},{4,5},{5,4},{6,7},{7,6},{8,9},{9,8},{10,11... | collective-permute-start | bytes 393224 | tf_op jit(solution)/shard_map/ppermute | solution.py:174
  3.8 3.3 %collective-permute-start.6 = (bf16[64,8,128]{2,1,0:T(8,128)(2,1)S(1)}, bf16[64,8,128]{2,1,0:T(8,128)(2,1)S(1)}, u32[]{:S(2)}, u32[]{:S(2)}) collective-permute-start(bf16[64,8,128]{2,1,0:T(8,128)(2,1)S(1)} %get-tuple-element.26), channel_id=1, source_target_pairs={{0,2},{1,3},{2,0},{3,1},{4,6},{5,7},{6,4},{7,5},{8,10},{9,11},{10,... | collective-permute-start | bytes 393224 | tf_op jit(solution)/shard_map/ppermute | solution.py:174
  7.1 1.2 %copy-done = bf16[1,128,16,256]{3,2,1,0:T(8,128)(2,1)S(1)} copy-done((bf16[1,128,16,256]{3,2,1,0:T(8,128)(2,1)S(1)}, bf16[1,128,16,256]{3,2,1,0:T(8,128)(2,1)}, u32[]{:S(2)}) %copy-start) | copy-done | bytes 1048600
  8.6 2.5 %collective-permute-start = (bf16[128,256]{1,0:T(8,128)(2,1)S(1)}, bf16[128,256]{1,0:T(8,128)(2,1)S(1)}, u32[]{:S(2)}, u32[]{:S(2)}) collective-permute-start(bf16[128,256]{1,0:T(8,128)(2,1)S(1)} %get-tuple-element.18), channel_id=1, source_target_pairs={{0,1},{1,2},{2,3},{4,5},{5,6},{6,7},{8,9},{9,10},{10,11},{12,13},{... | collective-permute-start | bytes 196616 | tf_op jit(solution)/shard_map/ppermute | solution.py:202
  11.0 1.3 %collective-permute-start.1 = (bf16[128,256]{1,0:T(8,128)(2,1)S(1)}, bf16[128,256]{1,0:T(8,128)(2,1)S(1)}, u32[]{:S(2)}, u32[]{:S(2)}) collective-permute-start(bf16[128,256]{1,0:T(8,128)(2,1)S(1)} %get-tuple-element.19), channel_id=1, source_target_pairs={{1,0},{2,1},{3,2},{5,4},{6,5},{7,6},{9,8},{10,9},{11,10},{13,12},{... | collective-permute-start | bytes 196616 | tf_op jit(solution)/shard_map/ppermute | solution.py:203
  12.4 1.2 %copy-done.1 = bf16[1,128,16,256]{3,2,1,0:T(8,128)(2,1)S(1)} copy-done((bf16[1,128,16,256]{3,2,1,0:T(8,128)(2,1)S(1)}, bf16[1,128,16,256]{3,2,1,0:T(8,128)(2,1)}, u32[]{:S(2)}) %copy-start.1) | copy-done | bytes 1048600
  13.6 2.1 %shard_map.50 = (bf16[1152,1024]{1,0:T(8,128)(2,1)S(1)}, bf16[1152,1024]{1,0:T(8,128)(2,1)S(1)}) custom-call(bf16[2048,256]{1,0:T(8,128)(2,1)S(1)} %bitcast.30), custom_call_target="tpu_custom_call" | custom-call | flops 450000000 | bytes 5767168 | tf_op jit(solution)/shard_map/pallas_call | solution.py:148
  15.7 2.1 %collective-permute-done.1.bot_ref.refs_7_ = bf16[128,256]{1,0:T(8,128)(2,1)S(1)} collective-permute-done((bf16[128,256]{1,0:T(8,128)(2,1)S(1)}, bf16[128,256]{1,0:T(8,128)(2,1)S(1)}, u32[]{:S(2)}, u32[]{:S(2)}) %collective-permute-start.1) | collective-permute-done | bytes 65568 | tf_op jit(solution)/shard_map/ppermute | solution.py:203
  17.8 2.0 %shard_map.53 = (f32[1152,128]{1,0:T(8,128)S(1)}, bf16[256,1024]{1,0:T(8,128)(2,1)S(1)}, bf16[768,128]{1,0:T(8,128)(2,1)S(1)}) custom-call(s32[1]{0:T(128)} %bitcast.8.core_ref, s32[1]{0:T(128)} %bitcast.slab_ref, bf16[512,128]{1,0:T(8,128)(2,1)S(1)} %bitcast.34, bf16[512,128]{1,0:T(8,128)(2,1)S(1)} %bitcast.35, bf16[512,128]{1,0:T(8,128)(2,1)S(1)} %bitcast.36, ...), custom_call_target="tpu_custom_call" | custom-call | flops 300000000 | bytes 6684680 | tf_op jit(solution)/shard_map/pallas_call | solution.py:148
  19.9 1.6 %shard_map.54.keep_ref = f32[1152,128]{1,0:T(8,128)S(1)} custom-call(s32[1]{0:T(128)} %bitcast.8.core_ref, bf16[256,1024]{1,0:T(8,128)(2,1)S(1)} %get-tuple-element.29.m_ref, bf16[1152,1024]{1,0:T(8,128)(2,1)S(1)} %get-tuple-element.17.d_ref.refs_4_, bf16[1152,1024]{1,0:T(8,128)(2,1)S(1)} %get-tuple-element.28.refs_5_.e_ref, ...), custom_call_target="tpu_custom_call" | custom-call | flops 300000000 | bytes 6029316 | tf_op jit(solution)/shard_map/pallas_call | solution.py:148
  22.0 14.4 %all_to_all.15 = bf16[16,72,128]{2,1,0:T(8,128)(2,1)S(1)} all-to-all(bf16[16,72,128]{2,1,0:T(8,128)(2,1)S(1)} %bitcast.28), channel_id=1, replica_groups=mesh['zh'=2,'x'=4,'y'=4,'c'=2,'s'=4] {'x','y'}, dimensions={0} | all-to-all | bytes 589824 | tf_op jit(solution)/shard_map/all_to_all | solution.py:178
  36.4 17.4 %all_to_all.16 = bf16[8,72,128]{2,1,0:T(8,128)(2,1)S(1)} all-to-all(bf16[8,72,128]{2,1,0:T(8,128)(2,1)S(1)} %bitcast.32), channel_id=1, replica_groups=mesh['zh'=2,'x'=4,'y'=4,'c'=2,'s'=4] {'zh','s'}, dimensions={0} | all-to-all | bytes 294912 | tf_op jit(solution)/shard_map/all_to_all | solution.py:178
  53.8 0.7 shard_map.57
  54.6 6.2 %all-to-all-start.2 = ((bf16[16,72,128]{2,1,0:T(8,128)(2,1)}), bf16[16,72,128]{2,1,0:T(8,128)(2,1)}, u32[]{:S(2)}, u32[]{:S(2)}) async-start(bf16[16,72,128]{2,1,0:T(8,128)(2,1)} %bitcast.18), calls=%async_computation.2 | async-start | bytes 589824 | tf_op jit(solution)/shard_map/all_to_all | solution.py:178
  60.8 1.9 %shard_map.52 = (bf16[512,128]{1,0:T(8,128)(2,1)S(1)}, bf16[512,128]{1,0:T(8,128)(2,1)}, bf16[512,128]{1,0:T(8,128)(2,1)S(1)}, bf16[512,128]{1,0:T(8,128)(2,1)S(1)}) custom-call(s32[1]{0:T(128)} %bitcast.slab_ref, bf16[9,256,128]{2,1,0:T(8,128)(2,1)S(1)} %bitcast.31, bf16[1152,1024]{1,0:T(8,128)(2,1)S(1)} %get-tuple-element.17.d_ref.refs_4_, ...), custom_call_target="tpu_custom_call" | custom-call | flops 600000000 | bytes 3604484 | tf_op jit(solution)/shard_map/pallas_call | solution.py:148
  62.7 0.6 collective-permute-start.2
  63.2 0.5 collective-permute-start.3
  63.7 3.4 %collective-permute-start.4 = (bf16[512,128]{1,0:T(8,128)(2,1)S(1)}, bf16[512,128]{1,0:T(8,128)(2,1)S(1)}, u32[]{:S(2)}, u32[]{:S(2)}) collective-permute-start(bf16[512,128]{1,0:T(8,128)(2,1)S(1)} %get-tuple-element.23), channel_id=1, source_target_pairs={{0,3},{1,2},{2,1},{3,0},{4,7},{5,6},{6,5},{7,4},{8,11},{9,10},{10,... | collective-permute-start | bytes 393224 | tf_op jit(solution)/shard_map/ppermute | solution.py:174
  67.5 1.9 %collective-permute-done.2 = bf16[512,128]{1,0:T(8,128)(2,1)S(1)} collective-permute-done((bf16[512,128]{1,0:T(8,128)(2,1)}, bf16[512,128]{1,0:T(8,128)(2,1)S(1)}, u32[]{:S(2)}, u32[]{:S(2)}) %collective-permute-start.2) | collective-permute-done | bytes 131104 | tf_op jit(solution)/shard_map/ppermute | solution.py:174
  69.3 3.8 %collective-permute-done.3 = bf16[512,128]{1,0:T(8,128)(2,1)S(1)} collective-permute-done((bf16[512,128]{1,0:T(8,128)(2,1)S(1)}, bf16[512,128]{1,0:T(8,128)(2,1)S(1)}, u32[]{:S(2)}, u32[]{:S(2)}) %collective-permute-start.3) | collective-permute-done | bytes 131104 | tf_op jit(solution)/shard_map/ppermute | solution.py:174
  73.1 0.9 %copy_bitcast_fusion = bf16[1,64,32,128]{3,2,1,0:T(8,128)(2,1)} fusion(bf16[64,1,8,128]{3,2,0,1:T(8,128)(2,1)S(1)} %get-tuple-element.35, bf16[64,1,8,128]{3,2,0,1:T(8,128)(2,1)S(1)} %get-tuple-element.36, bf16[64,1,8,128]{3,2,0,1:T(8,128)(2,1)S(1)} %get-tuple-element.37, bf16[64,1,8,128]{3,2,0,1:T(8,128)(2,1)S(1)} %get-tuple-element.34), kind=kLoop, calls=%fused_computation.2 | loop fusion | flops 786432 | bytes 1048576 | tf_op jit(solution)/shard_map/reshape | solution.py:241
  74.0 1.0 %broadcast_select_fusion.1 = (bf16[9,128,128]{2,1,0:T(8,128)(2,1)S(1)}, bf16[9,128,128]{2,1,0:T(8,128)(2,1)S(1)}) fusion(bf16[9,128,128]{2,1,0:T(8,128)(2,1)} %bitcast.19, bf16[9,128,128]{2,1,0:T(8,128)(2,1)S(1)} %collective-permute-done.9, pred[]{:T(512)S(6)} %eq.51), kind=kLoop, calls=%fused_computation.4 | loop fusion | flops 294912 | bytes 1179649 | tf_op jit(solution)/shard_map/jit(_where)/select_n | solution.py:230
  75.1 1.1 %maximum_convert_fusion = f32[3,3,256,128]{3,2,1,0:T(8,128)} fusion(bf16[3,3,128,128]{3,2,1,0:T(8,128)(2,1)S(1)} %bitcast.39, bf16[3,3,128,128]{3,2,1,0:T(8,128)(2,1)S(1)} %bitcast.38), kind=kLoop, calls=%fused_computation | loop fusion | flops 1179648 | bytes 1769472 | tf_op jit(solution)/shard_map/convert_element_type | solution.py:242
  (19 shorter events, 1.4 us)
Async XLA Ops:
  1.8 16.0 %collective-permute-start.5 = (bf16[64,8,128]{2,1,0:T(8,128)(2,1)S(1)}, bf16[64,8,128]{2,1,0:T(8,128)(2,1)S(1)}, u32[]{:S(2)}, u32[]{:S(2)}) collective-permute-start(bf16[64,8,128]{2,1,0:T(8,128)(2,1)S(1)} %get-tuple-element.25), channel_id=1, source_target_pairs={{0,1},{1,0},{2,3},{3,2},{4,5},{5,4},{6,7},{7,6},{8,9},{9,8},{10,11... | collective-permute-start | bytes 393224 | tf_op jit(solution)/shard_map/ppermute | solution.py:174
  3.8 14.0 %collective-permute-start.6 = (bf16[64,8,128]{2,1,0:T(8,128)(2,1)S(1)}, bf16[64,8,128]{2,1,0:T(8,128)(2,1)S(1)}, u32[]{:S(2)}, u32[]{:S(2)}) collective-permute-start(bf16[64,8,128]{2,1,0:T(8,128)(2,1)S(1)} %get-tuple-element.26), channel_id=1, source_target_pairs={{0,2},{1,3},{2,0},{3,1},{4,6},{5,7},{6,4},{7,5},{8,10},{9,11},{10,... | collective-permute-start | bytes 393224 | tf_op jit(solution)/shard_map/ppermute | solution.py:174
  7.1 10.7 %collective-permute-start.7 = (bf16[64,8,128]{2,1,0:T(8,128)(2,1)S(1)}, bf16[64,8,128]{2,1,0:T(8,128)(2,1)S(1)}, u32[]{:S(2)}, u32[]{:S(2)}) collective-permute-start(bf16[64,8,128]{2,1,0:T(8,128)(2,1)S(1)} %get-tuple-element.27), channel_id=1, source_target_pairs={{0,3},{1,2},{2,1},{3,0},{4,7},{5,6},{6,5},{7,4},{8,11},{9,10},{10,... | collective-permute-start | bytes 393224 | tf_op jit(solution)/shard_map/ppermute | solution.py:174
  7.1 1.2 %copy-start = (bf16[1,128,16,256]{3,2,1,0:T(8,128)(2,1)S(1)}, bf16[1,128,16,256]{3,2,1,0:T(8,128)(2,1)}, u32[]{:S(2)}) copy-start(bf16[1,128,16,256]{3,2,1,0:T(8,128)(2,1)} %param.4) | copy-start | bytes 3145732
  8.6 7.1 %collective-permute-start = (bf16[128,256]{1,0:T(8,128)(2,1)S(1)}, bf16[128,256]{1,0:T(8,128)(2,1)S(1)}, u32[]{:S(2)}, u32[]{:S(2)}) collective-permute-start(bf16[128,256]{1,0:T(8,128)(2,1)S(1)} %get-tuple-element.18), channel_id=1, source_target_pairs={{0,1},{1,2},{2,3},{4,5},{5,6},{6,7},{8,9},{9,10},{10,11},{12,13},{... | collective-permute-start | bytes 196616 | tf_op jit(solution)/shard_map/ppermute | solution.py:202
  11.0 6.7 %collective-permute-start.1 = (bf16[128,256]{1,0:T(8,128)(2,1)S(1)}, bf16[128,256]{1,0:T(8,128)(2,1)S(1)}, u32[]{:S(2)}, u32[]{:S(2)}) collective-permute-start(bf16[128,256]{1,0:T(8,128)(2,1)S(1)} %get-tuple-element.19), channel_id=1, source_target_pairs={{1,0},{2,1},{3,2},{5,4},{6,5},{7,6},{9,8},{10,9},{11,10},{13,12},{... | collective-permute-start | bytes 196616 | tf_op jit(solution)/shard_map/ppermute | solution.py:203
  12.4 1.2 %copy-start.1 = (bf16[1,128,16,256]{3,2,1,0:T(8,128)(2,1)S(1)}, bf16[1,128,16,256]{3,2,1,0:T(8,128)(2,1)}, u32[]{:S(2)}) copy-start(bf16[1,128,16,256]{3,2,1,0:T(8,128)(2,1)} %param.4) | copy-start | bytes 3145732
  19.8 2.1 %collective-permute-start.8 = (f32[1152,128]{1,0:T(8,128)S(1)}, f32[1152,128]{1,0:T(8,128)S(1)}, u32[]{:S(2)}, u32[]{:S(2)}) collective-permute-start(f32[1152,128]{1,0:T(8,128)S(1)} %get-tuple-element.31), channel_id=1, source_target_pairs={{0,4},{4,0},{1,5},{5,1},{2,6},{6,2},{3,7},{7,3},{8,12},{12,8},{9,1... | collective-permute-start | bytes 1769480 | tf_op jit(solution)/shard_map/ppermute | solution.py:220
  21.9 38.8 %copy-start.2 = (bf16[3,3,256,128]{3,2,1,0:T(8,128)(2,1)S(1)}, bf16[3,3,256,128]{3,2,1,0:T(8,128)(2,1)}, u32[]{:S(2)}) copy-start(bf16[3,3,256,128]{3,2,1,0:T(8,128)(2,1)} %param.5) | copy-start | bytes 1769476
  54.6 12.9 %all-to-all-start.2 = ((bf16[16,72,128]{2,1,0:T(8,128)(2,1)}), bf16[16,72,128]{2,1,0:T(8,128)(2,1)}, u32[]{:S(2)}, u32[]{:S(2)}) async-start(bf16[16,72,128]{2,1,0:T(8,128)(2,1)} %bitcast.18), calls=%async_computation.2 | async-start | bytes 589824 | tf_op jit(solution)/shard_map/all_to_all | solution.py:178
  62.7 6.6 %collective-permute-start.2 = (bf16[512,128]{1,0:T(8,128)(2,1)}, bf16[512,128]{1,0:T(8,128)(2,1)S(1)}, u32[]{:S(2)}, u32[]{:S(2)}) collective-permute-start(bf16[512,128]{1,0:T(8,128)(2,1)} %get-tuple-element.21), channel_id=1, source_target_pairs={{0,1},{1,0},{2,3},{3,2},{4,5},{5,4},{6,7},{7,6},{8,9},{9,8},{10,11... | collective-permute-start | bytes 393224 | tf_op jit(solution)/shard_map/ppermute | solution.py:174
  63.2 9.8 %collective-permute-start.3 = (bf16[512,128]{1,0:T(8,128)(2,1)S(1)}, bf16[512,128]{1,0:T(8,128)(2,1)S(1)}, u32[]{:S(2)}, u32[]{:S(2)}) collective-permute-start(bf16[512,128]{1,0:T(8,128)(2,1)S(1)} %get-tuple-element.22), channel_id=1, source_target_pairs={{0,2},{1,3},{2,0},{3,1},{4,6},{5,7},{6,4},{7,5},{8,10},{9,11},{10,... | collective-permute-start | bytes 393224 | tf_op jit(solution)/shard_map/ppermute | solution.py:174
  63.7 9.4 %collective-permute-start.4 = (bf16[512,128]{1,0:T(8,128)(2,1)S(1)}, bf16[512,128]{1,0:T(8,128)(2,1)S(1)}, u32[]{:S(2)}, u32[]{:S(2)}) collective-permute-start(bf16[512,128]{1,0:T(8,128)(2,1)S(1)} %get-tuple-element.23), channel_id=1, source_target_pairs={{0,3},{1,2},{2,1},{3,0},{4,7},{5,6},{6,5},{7,4},{8,11},{9,10},{10,... | collective-permute-start | bytes 393224 | tf_op jit(solution)/shard_map/ppermute | solution.py:174
  67.5 6.6 %collective-permute-start.9 = (bf16[9,128,128]{2,1,0:T(8,128)(2,1)}, bf16[9,128,128]{2,1,0:T(8,128)(2,1)S(1)}, u32[]{:S(2)}, u32[]{:S(2)}) collective-permute-start(bf16[9,128,128]{2,1,0:T(8,128)(2,1)} %bitcast.19), channel_id=1, source_target_pairs={{0,4},{4,0},{1,5},{5,1},{2,6},{6,2},{3,7},{7,3},{8,12},{12,8},{9,1... | collective-permute-start | bytes 884744 | tf_op jit(solution)/shard_map/ppermute | solution.py:228
